TPU v7x, 512 devices: a whole 4x8x8 slice. The times are simulated.
512 devices in a mesh: rep: 8 (over y), exp: 64 (over x, z, core).
Axes of the slice: x: 4, y: 8, z: 8, core: 2. Of those that a mesh axis runs over, the one named last changes fastest.
Arguments:
- tokens: bfloat16 [65536, 1024], P(('rep', 'exp')), may hold values from -6 to 6
- cotangent: bfloat16 [65536, 1024], P(('rep', 'exp')), may hold values from -6 to 6
- expert_ids: int32 [65536, 2], P(('rep', 'exp')), may hold values from 0 to 63, all different within a row; in each aligned block of 128 rows (0 to 127, 128 to 255, ...) at most 8 rows name the same one
- combine_weight: float32 [65536, 2], P(('rep', 'exp')), may hold values from 0.2 to 1
- gate_weight: bfloat16 [64, 1024, 768], P('exp', 'rep'), may hold values from -0.1875 to 0.1875
- up_weight: bfloat16 [64, 1024, 768], P('exp', 'rep'), may hold values from -0.1875 to 0.1875
- down_weight: bfloat16 [64, 768, 1024], P('exp', None, 'rep'), may hold values from -0.21875 to 0.21875
Outputs:
- mixed: bfloat16 [65536, 1024], P(('rep', 'exp'))
- token_grad: bfloat16 [65536, 1024], P(('rep', 'exp'))
- gate_grad: bfloat16 [64, 1024, 768], P('exp', 'rep')
- up_grad: bfloat16 [64, 1024, 768], P('exp', 'rep')
- down_grad: bfloat16 [64, 768, 1024], P('exp', None, 'rep')
Inputs may be any that keep to these rules, and one draw needn't show every extreme that they name: `expert_ids`: each token names 2 different experts. Among the 128 tokens of one aligned block of rows, no expert is named more than 8 times, and in some block an expert is named exactly 8 times.
All inputs are finite; a program needn't handle non-finite values.
Results may differ from a plain program's by a relative error of at most 0.014.
Values may be sent and summed in bfloat16 or wider, within the bound.
No kernel may reach another device: no remote copies, remote signals or barrier semaphores. Data moves between devices by JAX's collectives and lax.ppermute only.
A program may use at most 64 MiB of HBM per device.

v0:
```python
import jax
import jax.numpy as jnp
from jax import lax
from jax.sharding import PartitionSpec as P


def slot_rows(block_ids, expert_count, capacity):
    flat = block_ids.reshape(-1)
    onehot = (flat[:, None] == jnp.arange(expert_count, dtype=jnp.int32)[None, :]).astype(jnp.int32)
    before = jnp.cumsum(onehot, axis=0) - onehot
    return flat * capacity + jnp.sum(before * onehot, axis=1)


def expert_forward(block_x, w_gate, w_up, w_down):
    gate_value = jnp.dot(block_x, w_gate, preferred_element_type=jnp.float32)
    up_value = jnp.dot(block_x, w_up, preferred_element_type=jnp.float32)
    swish_value = jax.nn.silu(gate_value)
    hidden = (swish_value * up_value).astype(jnp.bfloat16)
    output = jnp.dot(hidden, w_down, preferred_element_type=jnp.float32).astype(jnp.bfloat16)
    return (gate_value, up_value, swish_value, hidden, output)


def average_rows(received, replicas):
    features, hidden_units = received.shape
    stacked = received.reshape(replicas, features // replicas, hidden_units).astype(jnp.float32)
    return (jnp.sum(stacked, axis=0) / replicas).astype(jnp.bfloat16)


def per_device(tokens, cotangent, expert_ids, combine_weight, gate_weight, up_weight, down_weight):
    tok_rows, features = tokens.shape
    top_count = expert_ids.shape[1]
    groups = lax.axis_size("exp")
    replicas = lax.axis_size("rep")
    capacity = 2 * tok_rows * top_count // groups
    pair_count = tok_rows * top_count
    destination = slot_rows(expert_ids, groups, capacity)
    x_pairs = jnp.repeat(tokens, top_count, axis=0)
    cot_pairs = (combine_weight[:, :, None] * cotangent[:, None, :].astype(jnp.float32)).astype(
        jnp.bfloat16
    )
    cot_pairs = cot_pairs.reshape(pair_count, features)
    send_rows = jnp.zeros((groups * capacity, features), jnp.bfloat16).at[destination].set(x_pairs)
    send_cot = jnp.zeros((groups * capacity, features), jnp.bfloat16).at[destination].set(cot_pairs)
    w_gate, w_up, w_down = (
        lax.all_gather(gate_weight[0], "rep", axis=0, tiled=True),
        lax.all_gather(up_weight[0], "rep", axis=0, tiled=True),
        lax.all_gather(down_weight[0], "rep", axis=1, tiled=True),
    )
    recv_rows, recv_cot = (
        lax.all_to_all(send_rows, "exp", split_axis=0, concat_axis=0, tiled=True),
        lax.all_to_all(send_cot, "exp", split_axis=0, concat_axis=0, tiled=True),
    )
    gate_value, up_value, swish_value, hidden, output = expert_forward(
        recv_rows, w_gate, w_up, w_down
    )
    grad_hidden = lax.dot_general(
        recv_cot, w_down, (((1,), (1,)), ((), ())), preferred_element_type=jnp.float32
    )
    sigma = jax.nn.sigmoid(gate_value)
    grad_gate = (grad_hidden * up_value * sigma * (1.0 + gate_value * (1.0 - sigma))).astype(
        jnp.bfloat16
    )
    grad_up = (grad_hidden * swish_value).astype(jnp.bfloat16)
    grad_rows = (
        lax.dot_general(
            grad_gate, w_gate, (((1,), (1,)), ((), ())), preferred_element_type=jnp.float32
        )
        + lax.dot_general(
            grad_up, w_up, (((1,), (1,)), ((), ())), preferred_element_type=jnp.float32
        )
    ).astype(jnp.bfloat16)
    back_out, back_grad = (
        lax.all_to_all(output, "exp", split_axis=0, concat_axis=0, tiled=True),
        lax.all_to_all(grad_rows, "exp", split_axis=0, concat_axis=0, tiled=True),
    )
    part_gate = lax.dot_general(
        recv_rows, grad_gate, (((0,), (0,)), ((), ())), preferred_element_type=jnp.float32
    ).astype(jnp.bfloat16)
    part_up = lax.dot_general(
        recv_rows, grad_up, (((0,), (0,)), ((), ())), preferred_element_type=jnp.float32
    ).astype(jnp.bfloat16)
    part_down = lax.dot_general(
        recv_cot, hidden, (((0,), (0,)), ((), ())), preferred_element_type=jnp.float32
    ).astype(jnp.bfloat16)
    red_gate, red_up, red_down = (
        lax.all_to_all(part_gate, "rep", split_axis=0, concat_axis=0, tiled=True),
        lax.all_to_all(part_up, "rep", split_axis=0, concat_axis=0, tiled=True),
        lax.all_to_all(part_down, "rep", split_axis=0, concat_axis=0, tiled=True),
    )
    gate_grad = average_rows(red_gate, replicas)[None]
    up_grad = average_rows(red_up, replicas)[None]
    down_grad = average_rows(red_down, replicas).T[None]
    out_pairs = back_out[destination].reshape(tok_rows, top_count, features).astype(jnp.float32)
    mixed = jnp.sum(combine_weight[:, :, None] * out_pairs, axis=1).astype(jnp.bfloat16)
    grad_pairs = back_grad[destination].reshape(tok_rows, top_count, features).astype(jnp.float32)
    token_grad = jnp.sum(grad_pairs, axis=1).astype(jnp.bfloat16)
    return (mixed, token_grad, gate_grad, up_grad, down_grad)


def solution(mesh):
    placed = (
        P(("rep", "exp"), None),
        P(("rep", "exp"), None),
        P(("rep", "exp"), None),
        P(("rep", "exp"), None),
        P("exp", "rep", None),
        P("exp", "rep", None),
        P("exp", None, "rep"),
    )
    return jax.shard_map(
        per_device,
        mesh=mesh,
        in_specs=placed,
        out_specs=(
            P(("rep", "exp"), None),
            P(("rep", "exp"), None),
            P("exp", "rep", None),
            P("exp", "rep", None),
            P("exp", None, "rep"),
        ),
        check_vma=False,
    )
```

profile of v0, /device:TPU:1, one launch (start us, length us, event | category | flops | bytes accessed | tf_op | source)
XLA Modules:
  0.0 371.4 jit_solution(11726433471744356704)
XLA Ops:
  13.1 2.7 scatter_custom_fusion
  15.8 14.8 %all-to-all-start = ((bf16[64,8,1024]{2,1,0:T(8,128)(2,1)}), bf16[64,8,1024]{2,1,0:T(8,128)(2,1)S(1)}, u32[]{:S(2)}, u32[]{:S(2)}) async-start(bf16[64,8,1024]{2,1,0:T(8,128)(2,1)} %bitcast.3), calls=%async_computation | async-start | bytes 2097152 | tf_op jit(solution)/shard_map/all_to_all | solution.py:50
  32.7 2.8 scatter_custom_fusion.1
  35.5 23.7 %all-to-all-done = bf16[64,8,1024]{2,1,0:T(8,128)(2,1)S(1)} async-done(((bf16[64,8,1024]{2,1,0:T(8,128)(2,1)}), bf16[64,8,1024]{2,1,0:T(8,128)(2,1)S(1)}, u32[]{:S(2)}, u32[]{:S(2)}) %all-to-all-start) | async-done | bytes 1048608 | tf_op jit(solution)/shard_map/all_to_all | solution.py:50
  59.2 6.2 %all-to-all-start.2 = ((bf16[64,8,1024]{2,1,0:T(8,128)(2,1)}), bf16[64,8,1024]{2,1,0:T(8,128)(2,1)S(1)}, u32[]{:S(2)}, u32[]{:S(2)}) async-start(bf16[64,8,1024]{2,1,0:T(8,128)(2,1)} %bitcast.10), calls=%async_computation.2 | async-start | bytes 2097152 | tf_op jit(solution)/shard_map/all_to_all | solution.py:51
  65.4 3.5 fusion.5
  69.0 28.5 %all-gather.7.cloned.1.call-done = bf16[1,1024,768]{2,1,0:T(8,128)(2,1)} async-done(((bf16[1,128,768]{2,1,0:T(8,128)(2,1)}), bf16[1,1024,768]{2,1,0:T(8,128)(2,1)}) %all-gather.7.cloned.1.call-update) | async-done | bytes 1572880 | tf_op jit(solution)/shard_map/all_gather | solution.py:45
  97.5 3.5 fusion.9
  101.0 43.9 %all-gather.11.cloned.1.call-done = bf16[1,768,1024]{2,1,0:T(8,128)(2,1)} async-done(((bf16[1,768,128]{2,1,0:T(8,128)(2,1)}), bf16[1,768,1024]{2,1,0:T(8,128)(2,1)}) %all-gather.11.cloned.1.call-update) | async-done | bytes 1572880 | tf_op jit(solution)/shard_map/all_gather | solution.py:47
  145.0 4.9 %multiply_convert_fusion = (bf16[512,768]{1,0:T(8,128)(2,1)S(1)}, bf16[512,768]{1,0:T(8,128)(2,1)S(1)}, bf16[512,768]{1,0:T(8,128)(2,1)}) fusion(f32[512,768]{1,0:T(8,128)} %fusion.9, f32[512,768]{1,0:T(8,128)} %fusion.5, bf16[1,768,1024]{2,1,0:T(8,128)(2,1)} %all-gather.11.cloned.1.call-done, bf16[64,8,1024]{2,1,0:T(8,128)(2,1)S(1)} %all-to-all-done.2), kind=kOutput, calls=%fused_computation.22 | convolution fusion | flops 811204608 | bytes 8126464 | tf_op jit(solution)/shard_map/dot_general | solution.py:56
  153.9 15.0 %all-to-all-start.3 = ((bf16[64,8,1024]{2,1,0:T(8,128)(2,1)}), bf16[64,8,1024]{2,1,0:T(8,128)(2,1)S(1)}, u32[]{:S(2)}, u32[]{:S(2)}) async-start(bf16[64,8,1024]{2,1,0:T(8,128)(2,1)} %fusion.18), calls=%async_computation.3 | async-start | bytes 2097152 | tf_op jit(solution)/shard_map/all_to_all | solution.py:74
  168.9 3.4 fusion.15
  172.2 25.2 %all-to-all-done.3 = bf16[64,8,1024]{2,1,0:T(8,128)(2,1)S(1)} async-done(((bf16[64,8,1024]{2,1,0:T(8,128)(2,1)}), bf16[64,8,1024]{2,1,0:T(8,128)(2,1)S(1)}, u32[]{:S(2)}, u32[]{:S(2)}) %all-to-all-start.3) | async-done | bytes 1048608 | tf_op jit(solution)/shard_map/all_to_all | solution.py:74
  197.4 6.2 %all-to-all-start.1 = ((bf16[64,8,1024]{2,1,0:T(8,128)(2,1)}), bf16[64,8,1024]{2,1,0:T(8,128)(2,1)S(1)}, u32[]{:S(2)}, u32[]{:S(2)}) async-start(bf16[64,8,1024]{2,1,0:T(8,128)(2,1)} %fusion.15), calls=%async_computation.1 | async-start | bytes 2097152 | tf_op jit(solution)/shard_map/all_to_all | solution.py:73
  203.6 3.3 convolution_convert_fusion.2
  206.9 25.2 %all-to-all-done.1 = bf16[64,8,1024]{2,1,0:T(8,128)(2,1)S(1)} async-done(((bf16[64,8,1024]{2,1,0:T(8,128)(2,1)}), bf16[64,8,1024]{2,1,0:T(8,128)(2,1)S(1)}, u32[]{:S(2)}, u32[]{:S(2)}) %all-to-all-start.1) | async-done | bytes 1048608 | tf_op jit(solution)/shard_map/all_to_all | solution.py:73
  232.2 4.3 %all-to-all-start.4 = ((bf16[8,128,768]{2,1,0:T(8,128)(2,1)}), bf16[8,128,768]{2,1,0:T(8,128)(2,1)}, u32[]{:S(2)}, u32[]{:S(2)}) async-start(bf16[8,128,768]{2,1,0:T(8,128)(2,1)} %bitcast.89), calls=%async_computation.4 | async-start | bytes 3145728 | tf_op jit(solution)/shard_map/all_to_all | solution.py:86
  236.4 3.3 convolution_convert_fusion.1
  239.8 37.2 %all-to-all-done.4 = bf16[8,128,768]{2,1,0:T(8,128)(2,1)} async-done(((bf16[8,128,768]{2,1,0:T(8,128)(2,1)}), bf16[8,128,768]{2,1,0:T(8,128)(2,1)}, u32[]{:S(2)}, u32[]{:S(2)}) %all-to-all-start.4) | async-done | bytes 1572896 | tf_op jit(solution)/shard_map/all_to_all | solution.py:86
  277.0 4.4 %all-to-all-start.5 = ((bf16[8,128,768]{2,1,0:T(8,128)(2,1)}), bf16[8,128,768]{2,1,0:T(8,128)(2,1)}, u32[]{:S(2)}, u32[]{:S(2)}) async-start(bf16[8,128,768]{2,1,0:T(8,128)(2,1)} %bitcast.88), calls=%async_computation.5 | async-start | bytes 3145728 | tf_op jit(solution)/shard_map/all_to_all | solution.py:87
  281.4 3.3 convolution_convert_fusion
  284.7 34.9 %all-to-all-done.5 = bf16[8,128,768]{2,1,0:T(8,128)(2,1)} async-done(((bf16[8,128,768]{2,1,0:T(8,128)(2,1)}), bf16[8,128,768]{2,1,0:T(8,128)(2,1)}, u32[]{:S(2)}, u32[]{:S(2)}) %all-to-all-start.5) | async-done | bytes 1572896 | tf_op jit(solution)/shard_map/all_to_all | solution.py:87
  319.7 4.5 %all-to-all-start.6 = ((bf16[8,128,768]{2,1,0:T(8,128)(2,1)}), bf16[8,128,768]{2,1,0:T(8,128)(2,1)}, u32[]{:S(2)}, u32[]{:S(2)}) async-start(bf16[8,128,768]{2,1,0:T(8,128)(2,1)} %bitcast.87), calls=%async_computation.6 | async-start | bytes 3145728 | tf_op jit(solution)/shard_map/all_to_all | solution.py:88
  336.3 26.1 %all-to-all-done.6 = bf16[8,128,768]{2,1,0:T(8,128)(2,1)} async-done(((bf16[8,128,768]{2,1,0:T(8,128)(2,1)}), bf16[8,128,768]{2,1,0:T(8,128)(2,1)}, u32[]{:S(2)}, u32[]{:S(2)}) %all-to-all-start.6) | async-done | bytes 1572896 | tf_op jit(solution)/shard_map/all_to_all | solution.py:88
  (61 shorter events, 26.4 us)
Async XLA Ops:
  7.2 58.3 %all-gather.9.cloned.1.call-start = ((), (), s32[]{:S(2)}) async-start(), calls=%async_computation.8 | async-start | bytes 1769472 | tf_op jit(solution)/shard_map/all_gather | solution.py:46
  7.9 89.6 %all-gather.7.cloned.1.call-start = ((), (), s32[]{:S(2)}) async-start(), calls=%async_computation.7 | async-start | bytes 1769472 | tf_op jit(solution)/shard_map/all_gather | solution.py:45
  13.1 18.3 %copy-start.3 = (f32[128,2]{0,1:T(2,128)S(1)}, f32[128,2]{0,1:T(2,128)}, u32[]{:S(2)}) copy-start(f32[128,2]{0,1:T(2,128)} %param.10) | copy-start | bytes 3076
  13.1 18.6 %copy-start.2 = (bf16[128,1024]{1,0:T(8,128)(2,1)S(1)}, bf16[128,1024]{1,0:T(8,128)(2,1)}, u32[]{:S(2)}) copy-start(bf16[128,1024]{1,0:T(8,128)(2,1)} %param.8) | copy-start | bytes 786436
  15.8 43.4 %all-to-all-start = ((bf16[64,8,1024]{2,1,0:T(8,128)(2,1)}), bf16[64,8,1024]{2,1,0:T(8,128)(2,1)S(1)}, u32[]{:S(2)}, u32[]{:S(2)}) async-start(bf16[64,8,1024]{2,1,0:T(8,128)(2,1)} %bitcast.3), calls=%async_computation | async-start | bytes 2097152 | tf_op jit(solution)/shard_map/all_to_all | solution.py:50
  30.6 114.3 %all-gather.11.cloned.1.call-start = ((), (), s32[]{:S(2)}) async-start(), calls=%async_computation.9 | async-start | bytes 1769472 | tf_op jit(solution)/shard_map/all_gather | solution.py:47
  59.2 41.8 %all-to-all-start.2 = ((bf16[64,8,1024]{2,1,0:T(8,128)(2,1)}), bf16[64,8,1024]{2,1,0:T(8,128)(2,1)S(1)}, u32[]{:S(2)}, u32[]{:S(2)}) async-start(bf16[64,8,1024]{2,1,0:T(8,128)(2,1)} %bitcast.10), calls=%async_computation.2 | async-start | bytes 2097152 | tf_op jit(solution)/shard_map/all_to_all | solution.py:51
  101.0 48.9 %copy-start = (bf16[64,8,1024]{2,1,0:T(8,128)(2,1)}, bf16[64,8,1024]{2,1,0:T(8,128)(2,1)S(1)}, u32[]{:S(2)}) copy-start(bf16[64,8,1024]{2,1,0:T(8,128)(2,1)S(1)} %all-to-all-done.2) | copy-start | bytes 3145732
  145.0 4.9 %copy-start.5 = (bf16[1,1024,768]{2,1,0:T(8,128)(2,1)S(1)}, bf16[1,1024,768]{2,1,0:T(8,128)(2,1)}, u32[]{:S(2)}) copy-start(bf16[1,1024,768]{2,1,0:T(8,128)(2,1)} %all-gather.7.cloned.1.call-done) | copy-start | bytes 4718596
  149.9 1.0 copy-start.7
  149.9 1.1 copy-start.6
  149.9 2.0 copy-start.4
  153.9 15.0 %copy-start.8 = (bf16[512,768]{1,0:T(8,128)(2,1)S(1)}, bf16[512,768]{1,0:T(8,128)(2,1)}, u32[]{:S(2)}) copy-start(bf16[512,768]{1,0:T(8,128)(2,1)} %get-tuple-element.12) | copy-start | bytes 2359300
  153.9 43.5 %all-to-all-start.3 = ((bf16[64,8,1024]{2,1,0:T(8,128)(2,1)}), bf16[64,8,1024]{2,1,0:T(8,128)(2,1)S(1)}, u32[]{:S(2)}, u32[]{:S(2)}) async-start(bf16[64,8,1024]{2,1,0:T(8,128)(2,1)} %fusion.18), calls=%async_computation.3 | async-start | bytes 2097152 | tf_op jit(solution)/shard_map/all_to_all | solution.py:74
  197.4 34.8 %all-to-all-start.1 = ((bf16[64,8,1024]{2,1,0:T(8,128)(2,1)}), bf16[64,8,1024]{2,1,0:T(8,128)(2,1)S(1)}, u32[]{:S(2)}, u32[]{:S(2)}) async-start(bf16[64,8,1024]{2,1,0:T(8,128)(2,1)} %fusion.15), calls=%async_computation.1 | async-start | bytes 2097152 | tf_op jit(solution)/shard_map/all_to_all | solution.py:73
  232.2 44.8 %all-to-all-start.4 = ((bf16[8,128,768]{2,1,0:T(8,128)(2,1)}), bf16[8,128,768]{2,1,0:T(8,128)(2,1)}, u32[]{:S(2)}, u32[]{:S(2)}) async-start(bf16[8,128,768]{2,1,0:T(8,128)(2,1)} %bitcast.89), calls=%async_computation.4 | async-start | bytes 3145728 | tf_op jit(solution)/shard_map/all_to_all | solution.py:86
  277.0 4.5 %copy-start.1 = (bf16[64,8,1024]{2,1,0:T(8,128)(2,1)S(1)}, bf16[64,8,1024]{2,1,0:T(8,128)(2,1)}, u32[]{:S(2)}) copy-start(bf16[64,8,1024]{2,1,0:T(8,128)(2,1)} %copy-done) | copy-start | bytes 3145732
  277.0 42.7 %all-to-all-start.5 = ((bf16[8,128,768]{2,1,0:T(8,128)(2,1)}), bf16[8,128,768]{2,1,0:T(8,128)(2,1)}, u32[]{:S(2)}, u32[]{:S(2)}) async-start(bf16[8,128,768]{2,1,0:T(8,128)(2,1)} %bitcast.88), calls=%async_computation.5 | async-start | bytes 3145728 | tf_op jit(solution)/shard_map/all_to_all | solution.py:87
  319.7 42.7 %all-to-all-start.6 = ((bf16[8,128,768]{2,1,0:T(8,128)(2,1)}), bf16[8,128,768]{2,1,0:T(8,128)(2,1)}, u32[]{:S(2)}, u32[]{:S(2)}) async-start(bf16[8,128,768]{2,1,0:T(8,128)(2,1)} %bitcast.87), calls=%async_computation.6 | async-start | bytes 3145728 | tf_op jit(solution)/shard_map/all_to_all | solution.py:88
Sparse Core Ops, SparseCore 0:
  10.1 43.9 all-gather.8
  56.1 41.3 all-gather.6
  99.5 45.4 all-gather.10
where the time goes:
time: 372 us; the launch traced here: 371 us
  waiting for transfers between devices  247 us (66%)
  starting transfers between devices  55.5 us (15%)
  matrix products  28.3 us (8%)
  other arithmetic  14.8 us (4%)
  between operations  14 us (4%)
  local copies, waits for them, and re-layouts  11.9 us (3%)
    all_gather x1, waiting for transfers between devices, per_device(): lax.all_gather(down_weight[0], 'rep', axis=1, tiled=True)  43.9 us
    all_to_all x1, waiting for transfers between devices, per_device(): lax.all_to_all(part_gate, 'rep', split_axis=0, concat_axis=0, tiled=True)  37.2 us
    all_to_all x1, waiting for transfers between devices, per_device(): lax.all_to_all(part_up, 'rep', split_axis=0, concat_axis=0, tiled=True)  34.9 us
    all_gather x1, waiting for transfers between devices, per_device(): lax.all_gather(gate_weight[0], 'rep', axis=0, tiled=True)  28.5 us
    all_to_all x1, waiting for transfers between devices, per_device(): lax.all_to_all(part_down, 'rep', split_axis=0, concat_axis=0, tiled=True)  26.1 us
    all_to_all x1, waiting for transfers between devices, per_device(): lax.all_to_all(output, 'exp', split_axis=0, concat_axis=0, tiled=True)  25.2 us
    all_to_all x1, waiting for transfers between devices, per_device(): lax.all_to_all(grad_rows, 'exp', split_axis=0, concat_axis=0, tiled=True)  25.2 us
    all_to_all x1, waiting for transfers between devices, per_device(): lax.all_to_all(send_rows, 'exp', split_axis=0, concat_axis=0, tiled=True)  23.7 us
  transfers between devices with their start and end apart: 10, of which 8 were waited for; matrix products, arithmetic and copies ran while one was open for 12% of the time, Pallas kernels for 0%

commit v1 on v0

v1 whole, which is shorter than its diff:
```python
import jax
import jax.numpy as jnp
from jax import lax
from jax.experimental import pallas as pl
from jax.experimental.pallas import tpu as pltpu
from jax.sharding import PartitionSpec as P

F32 = jnp.float32
BF16 = jnp.bfloat16
VMEM_BYTES = 50 * 1024 * 1024


def nn(a, b):
    return lax.dot_general(a, b, (((1,), (0,)), ((), ())), preferred_element_type=F32)


def nt(a, b):
    return lax.dot_general(a, b, (((1,), (1,)), ((), ())), preferred_element_type=F32)


def tn(a, b):
    return lax.dot_general(a, b, (((0,), (0,)), ((), ())), preferred_element_type=F32)


def call(body, out_shape, name, **kw):
    return pl.pallas_call(
        body,
        out_shape=out_shape,
        name=name,
        compiler_params=pltpu.CompilerParams(vmem_limit_bytes=VMEM_BYTES),
        **kw,
    )


def pack_weights(gate_ref, up_ref, down_ref, out_ref):
    out_ref[0] = gate_ref[...]
    out_ref[1] = up_ref[...]
    out_ref[2] = down_ref[...].T


def slot_onehots(ids_ref, experts, capacity):
    top, rows = ids_ref.shape
    expert = lax.broadcasted_iota(jnp.int32, (experts, rows), 0)
    hot = [(ids_ref[k : k + 1, :] == expert).astype(F32) for k in range(top)]
    earlier = lax.broadcasted_iota(jnp.int32, (rows, rows), 0) < lax.broadcasted_iota(
        jnp.int32, (rows, rows), 1
    )
    before = nn(sum(hot).astype(BF16), earlier.astype(BF16))
    place = lax.broadcasted_iota(jnp.int32, (experts * capacity, rows), 0)
    picks = []
    for k in range(top):
        slot = jnp.sum(before * hot[k], axis=0, keepdims=True).astype(jnp.int32)
        picks.append(place == ids_ref[k : k + 1, :] * capacity + slot)
    return picks


def dispatch(experts, capacity):
    def body(ids_ref, cw_ref, tok_ref, cot_ref, out_ref):
        picks = slot_onehots(ids_ref, experts, capacity)
        row_weight = sum(
            jnp.sum(jnp.where(p, cw_ref[k : k + 1, :], 0.0), axis=1, keepdims=True)
            for k, p in enumerate(picks)
        )
        pick = (picks[0] | picks[1]).astype(BF16)
        features = tok_ref.shape[1]
        out_ref[:, 0] = nn(pick, tok_ref[...]).astype(BF16).reshape(experts, capacity, features)
        weighted = (nn(pick, cot_ref[...]) * row_weight).astype(BF16)
        out_ref[:, 1] = weighted.reshape(experts, capacity, features)

    return body


def expert_grads(xc_ref, w_ref, grads_ref, hidden_ref, dg_ref, du_ref):
    groups, _, capacity, features = xc_ref.shape
    reps, _, part, ff = w_ref.shape
    rows = groups * capacity
    x = xc_ref[:, 0].reshape(rows, features)
    c = xc_ref[:, 1].reshape(rows, features)
    gate = nn(x, w_ref[:, 0].reshape(features, ff))
    up = nn(x, w_ref[:, 1].reshape(features, ff))
    dh = nn(c, w_ref[:, 2].reshape(features, ff))
    sigma = jax.nn.sigmoid(gate)
    swish = gate * sigma
    hidden_ref[...] = (swish * up).astype(BF16)
    dg_ref[...] = (dh * up * sigma * (1.0 + gate * (1.0 - sigma))).astype(BF16)
    du_ref[...] = (dh * swish).astype(BF16)
    grads_ref[:, 0] = tn(x, dg_ref[...]).astype(BF16).reshape(reps, part, ff)
    grads_ref[:, 1] = tn(x, du_ref[...]).astype(BF16).reshape(reps, part, ff)
    grads_ref[:, 2] = tn(c, hidden_ref[...]).astype(BF16).reshape(reps, part, ff)


def expert_rows(w_ref, hidden_ref, dg_ref, du_ref, out_ref):
    groups, _, capacity, features = out_ref.shape
    ff = w_ref.shape[3]
    dx = nt(dg_ref[...], w_ref[:, 0].reshape(features, ff)) + nt(
        du_ref[...], w_ref[:, 1].reshape(features, ff)
    )
    out_ref[:, 1] = dx.astype(BF16).reshape(groups, capacity, features)
    o = nt(hidden_ref[...], w_ref[:, 2].reshape(features, ff))
    out_ref[:, 0] = o.astype(BF16).reshape(groups, capacity, features)


def combine(ids_ref, cw_ref, back_ref, mixed_ref, grad_ref):
    experts, _, capacity, features = back_ref.shape
    top, rows = ids_ref.shape
    picks = [p.astype(BF16) for p in slot_onehots(ids_ref, experts, capacity)]
    o = back_ref[:, 0].reshape(experts * capacity, features)
    dx = back_ref[:, 1].reshape(experts * capacity, features)
    column = jnp.concatenate([cw_ref[...], jnp.zeros((8 - top, rows), F32)], axis=0).T
    mixed = sum(column[:, k : k + 1] * tn(p, o) for k, p in enumerate(picks))
    mixed_ref[...] = mixed.astype(BF16)
    grad_ref[...] = tn(picks[0] + picks[1], dx).astype(BF16)


def finish_grads(replicas):
    def body(red_ref, gate_ref, up_ref, down_ref):
        gate_ref[...] = (red_ref[0].astype(F32) / replicas).astype(BF16)
        up_ref[...] = (red_ref[1].astype(F32) / replicas).astype(BF16)
        down_ref[...] = (red_ref[2].astype(F32) / replicas).astype(BF16).T

    return body


def per_device(tokens, cotangent, expert_ids, combine_weight, gate_weight, up_weight, down_weight):
    tok_rows, features = tokens.shape
    groups = lax.axis_size("exp")
    replicas = lax.axis_size("rep")
    _, part, ff = gate_weight.shape
    capacity = 2 * tok_rows * expert_ids.shape[1] // groups
    rows = groups * capacity
    ids, cw = expert_ids.T, combine_weight.T
    sds = jax.ShapeDtypeStruct

    packed = call(pack_weights, sds((3, part, ff), BF16), "pack_weights")(
        gate_weight[0], up_weight[0], down_weight[0]
    )
    weights = lax.all_gather(packed, "rep", axis=0)
    wire = (groups, 2, capacity, features)
    sent = call(dispatch(groups, capacity), sds(wire, BF16), "dispatch")(
        ids, cw, tokens, cotangent
    )
    received = lax.all_to_all(sent, "exp", split_axis=0, concat_axis=0, tiled=True)
    grads, hidden, dg, du = call(
        expert_grads,
        (sds((replicas, 3, part, ff), BF16),) + (sds((rows, ff), BF16),) * 3,
        "expert_grads",
    )(received, weights)
    reduced = lax.psum_scatter(grads, "rep", scatter_dimension=0)
    results = call(expert_rows, sds(wire, BF16), "expert_rows")(weights, hidden, dg, du)
    back = lax.all_to_all(results, "exp", split_axis=0, concat_axis=0, tiled=True)
    mixed, token_grad = call(combine, (sds((tok_rows, features), BF16),) * 2, "combine")(
        ids, cw, back
    )
    gate_grad, up_grad, down_grad = call(
        finish_grads(replicas),
        (sds((part, ff), BF16), sds((part, ff), BF16), sds((ff, part), BF16)),
        "finish_grads",
    )(reduced)
    return (mixed, token_grad, gate_grad[None], up_grad[None], down_grad[None])


def solution(mesh):
    placed = (
        P(("rep", "exp"), None),
        P(("rep", "exp"), None),
        P(("rep", "exp"), None),
        P(("rep", "exp"), None),
        P("exp", "rep", None),
        P("exp", "rep", None),
        P("exp", None, "rep"),
    )
    return jax.shard_map(
        per_device,
        mesh=mesh,
        in_specs=placed,
        out_specs=(
            P(("rep", "exp"), None),
            P(("rep", "exp"), None),
            P("exp", "rep", None),
            P("exp", "rep", None),
            P("exp", None, "rep"),
        ),
        check_vma=False,
    )
```

time: 372 us -> 169 us (0.45)
  waiting for transfers between devices: 247 us -> 0.04 us
  blocking collectives: 0 us -> 126 us
  starting transfers between devices: 55.5 us -> 0.08 us
  matrix products: 28.3 us -> 0 us
  Pallas kernels: 0 us -> 21.1 us
  other arithmetic: 14.8 us -> 0 us
  local copies, waits for them, and re-layouts: 11.9 us -> 7.1 us
    all_to_all x7 -> x0, waiting for transfers between devices: 172 us -> none  [the longest x1 37.2 us: per_device(): lax.all_to_all(part_gate, 'rep', split_axis=0, concat_axis=0, tiled=True)]
    all_to_all x0 -> x2, blocking collectives: none -> 126 us  [the longest x1 65.8 us: per_device(): lax.all_to_all(sent, 'exp', split_axis=0, concat_axis=0, tiled=True)]
    all_gather x3 -> x1, waiting for transfers between devices: 72.4 us -> 0.01 us  [per_device(): weights = lax.all_gather(packed, 'rep', axis=0)]
    all_to_all x7 -> x0, starting transfers between devices: 55.4 us -> none  [the longest x1 15 us: per_device(): lax.all_to_all(grad_rows, 'exp', split_axis=0, concat_axis=0, tiled=True)]
    dot_general x9 -> x0, matrix products: 28.3 us -> none  [the longest x1 4.92 us: per_device(): lax.dot_general(recv_cot, w_down, (((1,), (1,)), ((), ())), preferred_ele...]
    pallas_call x0 -> x6, Pallas kernels: none -> 21.1 us  [the longest x1 10.6 us: per_device(): call(expert_grads, (sds((replicas, 3, part, ff), BF16),) + (sds((rows, ff...]
    reduce_sum x6 -> x0, other arithmetic: 9.24 us -> none  [the longest x3 4.98 us: average_rows(): return (jnp.sum(stacked, axis=0) / replicas).astype(jnp.bfloat16)]
    unnamed x21 -> x20, local copies, waits for them, and re-layouts: 2.69 us -> 7.1 us
  transfers between devices with their start and end apart: 10 -> 2, of which waited for: 8 -> 0; matrix products, arithmetic and copies ran while one was open for 12% -> 0% of each run, Pallas kernels for 0% -> 5%
where the time goes in v1:
time: 169 us; the launch traced here: 168 us
  blocking collectives  126 us (75%)
  Pallas kernels  21.1 us (12%)
  between operations  14.1 us (8%)
  local copies, waits for them, and re-layouts  7.1 us (4%)
    all_to_all x1, blocking collectives, per_device(): lax.all_to_all(sent, 'exp', split_axis=0, concat_axis=0, tiled=True)  65.8 us
    all_to_all x1, blocking collectives, per_device(): lax.all_to_all(results, 'exp', split_axis=0, concat_axis=0, tiled=True)  60.1 us
    pallas_call x1, Pallas kernels, per_device(): call(expert_grads, (sds((replicas, 3, part, ff), BF16),) + (sds((rows, ff...  10.6 us
    unnamed x20, local copies, waits for them, and re-layouts  7.1 us
    pallas_call x1, Pallas kernels, per_device(): call(expert_rows, sds(wire, BF16), 'expert_rows')(weights, hidden, dg, du)  6.29 us
  transfers between devices with their start and end apart: 2, of which 0 were waited for; matrix products, arithmetic and copies ran while one was open for 0% of the time, Pallas kernels for 5%

profile of v1, /device:TPU:1, one launch (start us, length us, event | category | flops | bytes accessed | tf_op | source)
XLA Modules:
  0.0 168.3 jit_solution(1200418243872056385)
XLA Ops:
  7.2 0.0 all-gather.3.cloned.1.call-start
  7.2 0.0 copy-start.3
  7.2 0.9 copy-done.3
  8.1 0.9 copy-done.4
  9.1 0.9 copy-done.5
  10.0 0.9 pack_weights.1
  10.9 0.0 all-gather.3.cloned.1.call-update
  10.9 0.0 reduce-scatter.2.cloned.1.call-start
  11.0 0.0 copy-start.1
  11.0 0.9 copy-done.1
  11.9 0.9 copy-done.2
  12.9 0.7 copy-done.6
  13.6 0.7 copy-done.8
  14.3 0.9 dispatch.1
  15.1 65.8 %all_to_all.10.xc_ref = bf16[64,2,8,1024]{3,2,1,0:T(8,128)(2,1)} all-to-all(bf16[64,2,8,1024]{3,2,1,0:T(8,128)(2,1)S(1)} %dispatch.1), channel_id=1, replica_groups=mesh['rep'=8,'exp'=64] {'exp'}, dimensions={0} | all-to-all | bytes 4194304 | tf_op jit(solution)/shard_map/all_to_all | solution.py:142
  80.9 10.6 %expert_grads.1 = (bf16[8,3,128,768]{3,2,1,0:T(8,128)(2,1)}, bf16[512,768]{1,0:T(8,128)(2,1)S(1)}, bf16[512,768]{1,0:T(8,128)(2,1)S(1)}, bf16[512,768]{1,0:T(8,128)(2,1)S(1)}) custom-call(bf16[64,2,8,1024]{3,2,1,0:T(8,128)(2,1)} %all_to_all.10.xc_ref, bf16[8,3,128,768]{3,2,1,0:T(8,128)(2,1)} %bitcast.18), custom_call_target="tpu_custom_call" | custom-call | tf_op jit(solution)/shard_map/expert_grads/pallas_call | solution.py:143
  91.5 0.0 reduce-scatter.2.cloned.1.call-update
  91.5 6.3 %expert_rows.1 = bf16[64,2,8,1024]{3,2,1,0:T(8,128)(2,1)} custom-call(bf16[8,3,128,768]{3,2,1,0:T(8,128)(2,1)} %bitcast.19, bf16[512,768]{1,0:T(8,128)(2,1)S(1)} %get-tuple-element.14.hidden_ref, bf16[512,768]{1,0:T(8,128)(2,1)S(1)} %get-tuple-element.15.dg_ref, bf16[512,768]{1,0:T(8,128)(2,1)S(1)} %get-tuple-element.16.du_ref), custom_call_target="tpu_custom_call" | custom-call | tf_op jit(solution)/shard_map/expert_rows/pallas_call | solution.py:149
  97.8 60.1 %all_to_all.11.back_ref = bf16[64,2,8,1024]{3,2,1,0:T(8,128)(2,1)S(1)} all-to-all(bf16[64,2,8,1024]{3,2,1,0:T(8,128)(2,1)} %expert_rows.1), channel_id=1, replica_groups=mesh['rep'=8,'exp'=64] {'exp'}, dimensions={0} | all-to-all | bytes 4194304 | tf_op jit(solution)/shard_map/all_to_all | solution.py:150
  157.9 0.0 copy-done.7
  157.9 0.0 copy-done.9
  157.9 1.5 combine.1
  159.5 1.1 copy-done
  160.5 0.9 finish_grads.1
  (10 shorter events, 0.0 us)
Async XLA Ops:
  7.2 73.8 %all-gather.3.cloned.1.call-start = ((), (), s32[]{:S(2)}) async-start(), calls=%async_computation.4 | async-start | bytes 5308416 | tf_op jit(solution)/shard_map/all_gather | solution.py:137
  7.2 0.9 copy-start.3
  8.1 0.9 copy-start.4
  9.1 0.9 copy-start.5
  10.9 148.5 %reduce-scatter.2.cloned.1.call-start = ((), (), s32[]{:S(2)}) async-start(), calls=%async_computation.3 | async-start | bytes 5308416 | tf_op jit(solution)/shard_map/reduce_scatter | solution.py:148
  11.0 1.0 copy-start.1
  11.9 0.9 copy-start.2
  12.9 0.7 copy-start.6
  13.6 0.7 copy-start.8
  97.8 60.1 %copy-start.7 = (s32[128,2]{0,1:T(2,128)S(1)}, s32[128,2]{0,1:T(2,128)}, u32[]{:S(2)}) copy-start(s32[128,2]{0,1:T(2,128)} %param.9) | copy-start | bytes 3076
  97.8 60.1 %copy-start.9 = (f32[128,2]{0,1:T(2,128)S(1)}, f32[128,2]{0,1:T(2,128)}, u32[]{:S(2)}) copy-start(f32[128,2]{0,1:T(2,128)} %param.10) | copy-start | bytes 3076
  159.4 1.1 copy-start
Sparse Core Ops, SparseCore 0:
  11.1 67.5 all-gather.2
  91.6 59.3 reduce-scatter.1

commit v2 on v1

v2 whole, which is shorter than its diff:
```python
import jax
import jax.numpy as jnp
from jax import lax
from jax.experimental import pallas as pl
from jax.experimental.pallas import tpu as pltpu
from jax.sharding import PartitionSpec as P

F32 = jnp.float32
BF16 = jnp.bfloat16
VMEM_BYTES = 50 * 1024 * 1024


def nn(a, b):
    return lax.dot_general(a, b, (((1,), (0,)), ((), ())), preferred_element_type=F32)


def nt(a, b):
    return lax.dot_general(a, b, (((1,), (1,)), ((), ())), preferred_element_type=F32)


def tn(a, b):
    return lax.dot_general(a, b, (((0,), (0,)), ((), ())), preferred_element_type=F32)


HBM = pl.BlockSpec(memory_space=pltpu.HBM)
VMEM = pl.BlockSpec(memory_space=pltpu.VMEM)
copy = pltpu.make_async_copy


def call(body, out_shape, name, **kw):
    return pl.pallas_call(
        body,
        out_shape=out_shape,
        name=name,
        compiler_params=pltpu.CompilerParams(vmem_limit_bytes=VMEM_BYTES),
        **kw,
    )


def in_hbm(*arrays):
    return [pltpu.with_memory_space_constraint(a, pltpu.HBM) for a in arrays]


def run(copies):
    for c in copies:
        c.start()
    return copies


def drain(copies):
    for c in copies:
        c.wait()


def pack_weights(gate_hbm, up_hbm, down_hbm, out_hbm, down, turned, sems):
    fetch = copy(down_hbm, down, sems.at[0])
    fetch.start()
    rest = run([copy(gate_hbm, out_hbm.at[0], sems.at[1]), copy(up_hbm, out_hbm.at[1], sems.at[2])])
    fetch.wait()
    turned[...] = down[...].T
    rest += run([copy(turned, out_hbm.at[2], sems.at[3])])
    drain(rest)


def slot_onehots(ids_ref, experts, capacity):
    top, rows = ids_ref.shape
    expert = lax.broadcasted_iota(jnp.int32, (experts, rows), 0)
    hot = [(ids_ref[k : k + 1, :] == expert).astype(F32) for k in range(top)]
    earlier = lax.broadcasted_iota(jnp.int32, (rows, rows), 0) < lax.broadcasted_iota(
        jnp.int32, (rows, rows), 1
    )
    before = nn(sum(hot).astype(BF16), earlier.astype(BF16))
    place = lax.broadcasted_iota(jnp.int32, (experts * capacity, rows), 0)
    picks = []
    for k in range(top):
        slot = jnp.sum(before * hot[k], axis=0, keepdims=True).astype(jnp.int32)
        picks.append(place == ids_ref[k : k + 1, :] * capacity + slot)
    return picks


def dispatch(experts, capacity):
    def body(ids_hbm, cw_hbm, tok_hbm, cot_hbm, out_ref, ids_ref, cw_ref, tok, cot, sems):
        small = run([copy(ids_hbm, ids_ref, sems.at[2]), copy(cw_hbm, cw_ref, sems.at[3])])
        fetch = run([copy(tok_hbm, tok, sems.at[0]), copy(cot_hbm, cot, sems.at[1])])
        drain(small)
        picks = slot_onehots(ids_ref, experts, capacity)
        row_weight = sum(
            jnp.sum(jnp.where(p, cw_ref[k : k + 1, :], 0.0), axis=1, keepdims=True)
            for k, p in enumerate(picks)
        )
        pick = (picks[0] | picks[1]).astype(BF16)
        features = tok.shape[1]
        fetch[0].wait()
        out_ref[:, 0] = nn(pick, tok[...]).astype(BF16).reshape(experts, capacity, features)
        fetch[1].wait()
        weighted = (nn(pick, cot[...]) * row_weight).astype(BF16)
        out_ref[:, 1] = weighted.reshape(experts, capacity, features)

    return body


def experts_step(
    xc_ref, w_hbm, grads_hbm, out_hbm, w, g, out, hidden, dg, du, in_sems, grad_sems, out_sems
):
    groups, _, capacity, features = xc_ref.shape
    reps, _, part, ff = w_hbm.shape
    rows = groups * capacity
    fetch = run([copy(w_hbm.at[:, i], w.at[i], in_sems.at[i]) for i in range(3)])
    weight = lambda i: w[i].reshape(features, ff)
    x = lambda: xc_ref[:, 0].reshape(rows, features)
    c = lambda: xc_ref[:, 1].reshape(rows, features)
    fetch[0].wait()
    gate = nn(x(), weight(0))
    fetch[1].wait()
    up = nn(x(), weight(1))
    fetch[2].wait()
    dh = nn(c(), weight(2))
    sigma = jax.nn.sigmoid(gate)
    swish = gate * sigma
    hidden[...] = (swish * up).astype(BF16)
    dg[...] = (dh * up * sigma * (1.0 + gate * (1.0 - sigma))).astype(BF16)
    du[...] = (dh * swish).astype(BF16)
    pending = []
    half = reps // 2
    for i, (left, right) in enumerate(((x, dg), (x, du), (c, hidden))):
        for h in range(2):
            block = slice(h * half, (h + 1) * half)
            cols = slice(h * half * part, (h + 1) * half * part)
            g[i, block] = tn(left()[:, cols], right[...]).astype(BF16).reshape(half, part, ff)
            pending += run([copy(g.at[i, block], grads_hbm.at[block, i], grad_sems.at[i, h])])
    half = groups // 2
    for h in range(2):
        block = slice(h * half, (h + 1) * half)
        some = slice(h * half * capacity, (h + 1) * half * capacity)
        dx = nt(dg[some], weight(0)) + nt(du[some], weight(1))
        out[block, 1] = dx.astype(BF16).reshape(half, capacity, features)
        pending += run([copy(out.at[block, 1], out_hbm.at[block, 1], out_sems.at[1, h])])
        o = nt(hidden[some], weight(2))
        out[block, 0] = o.astype(BF16).reshape(half, capacity, features)
        pending += run([copy(out.at[block, 0], out_hbm.at[block, 0], out_sems.at[0, h])])
    drain(pending)


def finish(replicas):
    def body(
        ids_ref, cw_ref, back_ref, red_hbm, mixed_ref, grad_ref, gate_ref, up_ref, down_ref, red, sems
    ):
        fetch = run([copy(red_hbm, red, sems.at[0])])
        experts, _, capacity, features = back_ref.shape
        top, rows = ids_ref.shape
        picks = [p.astype(BF16) for p in slot_onehots(ids_ref, experts, capacity)]
        o = back_ref[:, 0].reshape(experts * capacity, features)
        dx = back_ref[:, 1].reshape(experts * capacity, features)
        column = jnp.concatenate([cw_ref[...], jnp.zeros((8 - top, rows), F32)], axis=0).T
        mixed = sum(column[:, k : k + 1] * tn(p, o) for k, p in enumerate(picks))
        mixed_ref[...] = mixed.astype(BF16)
        grad_ref[...] = tn(picks[0] + picks[1], dx).astype(BF16)
        drain(fetch)
        gate_ref[...] = (red[0].astype(F32) / replicas).astype(BF16)
        up_ref[...] = (red[1].astype(F32) / replicas).astype(BF16)
        down_ref[...] = (red[2].astype(F32) / replicas).astype(BF16).T

    return body


def per_device(tokens, cotangent, expert_ids, combine_weight, gate_weight, up_weight, down_weight):
    tok_rows, features = tokens.shape
    groups = lax.axis_size("exp")
    replicas = lax.axis_size("rep")
    _, part, ff = gate_weight.shape
    capacity = 2 * tok_rows * expert_ids.shape[1] // groups
    rows = groups * capacity
    ids, cw = expert_ids.T, combine_weight.T
    sds = jax.ShapeDtypeStruct

    sems = pltpu.SemaphoreType.DMA
    scratch = pltpu.VMEM
    packed = call(
        pack_weights,
        pltpu.HBM((3, part, ff), BF16),
        "pack_weights",
        in_specs=[HBM] * 3,
        out_specs=HBM,
        scratch_shapes=[scratch((ff, part), BF16), scratch((part, ff), BF16), sems((4,))],
    )(*in_hbm(gate_weight[0], up_weight[0], down_weight[0]))
    weights = lax.all_gather(packed, "rep", axis=0)
    wire = (groups, 2, capacity, features)
    sent = call(
        dispatch(groups, capacity),
        sds(wire, BF16),
        "dispatch",
        in_specs=[HBM] * 4,
        out_specs=VMEM,
        scratch_shapes=[scratch(ids.shape, jnp.int32), scratch(cw.shape, F32)]
        + [scratch(tokens.shape, BF16)] * 2
        + [sems((4,))],
    )(*in_hbm(ids, cw, tokens, cotangent))
    received = lax.all_to_all(sent, "exp", split_axis=0, concat_axis=0, tiled=True)
    grads, results = call(
        experts_step,
        (pltpu.HBM((replicas, 3, part, ff), BF16), pltpu.HBM(wire, BF16)),
        "experts_step",
        in_specs=[VMEM, HBM],
        out_specs=(HBM, HBM),
        scratch_shapes=[
            scratch((3, replicas, part, ff), BF16),
            scratch((3, replicas, part, ff), BF16),
            scratch(wire, BF16),
        ]
        + [scratch((rows, ff), BF16)] * 3
        + [sems((3,)), sems((3, 2)), sems((2, 2))],
    )(received, *in_hbm(weights))
    reduced = lax.psum_scatter(grads, "rep", scatter_dimension=0)
    back = lax.all_to_all(results, "exp", split_axis=0, concat_axis=0, tiled=True)
    mixed, token_grad, gate_grad, up_grad, down_grad = call(
        finish(replicas),
        (sds((tok_rows, features), BF16),) * 2
        + (sds((part, ff), BF16), sds((part, ff), BF16), sds((ff, part), BF16)),
        "finish",
        in_specs=[VMEM, VMEM, VMEM, HBM],
        out_specs=(VMEM,) * 5,
        scratch_shapes=[scratch((3, part, ff), BF16), sems((1,))],
    )(ids, cw, back, *in_hbm(reduced))
    return (mixed, token_grad, gate_grad[None], up_grad[None], down_grad[None])


def solution(mesh):
    placed = (
        P(("rep", "exp"), None),
        P(("rep", "exp"), None),
        P(("rep", "exp"), None),
        P(("rep", "exp"), None),
        P("exp", "rep", None),
        P("exp", "rep", None),
        P("exp", None, "rep"),
    )
    return jax.shard_map(
        per_device,
        mesh=mesh,
        in_specs=placed,
        out_specs=(
            P(("rep", "exp"), None),
            P(("rep", "exp"), None),
            P("exp", "rep", None),
            P("exp", "rep", None),
            P("exp", None, "rep"),
        ),
        check_vma=False,
    )
```

time: 169 us -> 171 us (1.012)
  Pallas kernels: 21.1 us -> 28.9 us
  local copies, waits for them, and re-layouts: 7.1 us -> 0.01 us
  blocking collectives: 126 us -> 128 us
    pallas_call x6 -> x4, Pallas kernels: 21.1 us -> 28.9 us  [the longest x1 13.1 us: per_device(): call(pack_weights, pltpu.HBM((3, part, ff), BF16), 'pack_weights', in_spe...]
    unnamed x20 -> x4, local copies, waits for them, and re-layouts: 7.1 us -> 0.01 us
    all_to_all x1, blocking collectives: 60.1 us -> 62.1 us  [per_device(): lax.all_to_all(results, 'exp', split_axis=0, concat_axis=0, tiled=True)]
  transfers between devices with their start and end apart: 2 -> 2, of which waited for: 0 -> 0; matrix products, arithmetic and copies ran while one was open for 0% -> 0% of each run, Pallas kernels for 5% -> 1%
where the time goes in v2:
time: 171 us
  blocking collectives  128 us (75%)
  Pallas kernels  28.9 us (17%)
  between operations  14.1 us (8%)
    all_to_all x1, blocking collectives, per_device(): lax.all_to_all(sent, 'exp', split_axis=0, concat_axis=0, tiled=True)  65.9 us
    all_to_all x1, blocking collectives, per_device(): lax.all_to_all(results, 'exp', split_axis=0, concat_axis=0, tiled=True)  62.1 us
    pallas_call x1, Pallas kernels, per_device(): call(pack_weights, pltpu.HBM((3, part, ff), BF16), 'pack_weights', in_spe...  13.1 us
    pallas_call x1, Pallas kernels, per_device(): call(experts_step, (pltpu.HBM((replicas, 3, part, ff), BF16), pltpu.HBM(w...  11.1 us
  transfers between devices with their start and end apart: 2, of which 0 were waited for; matrix products, arithmetic and copies ran while one was open for 0% of the time, Pallas kernels for 1%

profile of v2, /device:TPU:1, one launch (start us, length us, event | category | flops | bytes accessed | tf_op | source)
XLA Modules:
  0.0 171.1 jit_solution(3443275748369986073)
XLA Ops:
  7.2 0.0 all-gather.3.cloned.1.call-start
  7.2 13.1 %pack_weights.1 = bf16[3,128,768]{2,1,0:T(8,128)(2,1)} custom-call(bf16[128,768]{1,0:T(8,128)(2,1)} %bitcast.16, bf16[128,768]{1,0:T(8,128)(2,1)} %bitcast.17, bf16[768,128]{1,0:T(8,128)(2,1)} %bitcast.18), custom_call_target="tpu_custom_call" | custom-call | tf_op jit(solution)/shard_map/pack_weights/pallas_call | solution.py:178
  20.3 0.0 all-gather.3.cloned.1.call-update
  20.3 0.0 reduce-scatter.2.cloned.1.call-start
  20.3 2.0 %dispatch.1 = bf16[64,2,8,1024]{3,2,1,0:T(8,128)(2,1)S(1)} custom-call(s32[2,128]{1,0:T(2,128)} %bitcast.10, f32[2,128]{1,0:T(2,128)} %bitcast.12, bf16[128,1024]{1,0:T(8,128)(2,1)} %tok_hbm.1, bf16[128,1024]{1,0:T(8,128)(2,1)} %cot_hbm.1), custom_call_target="tpu_custom_call" | custom-call | tf_op jit(solution)/shard_map/dispatch/pallas_call | solution.py:188
  22.4 65.9 %all_to_all.10.xc_ref = bf16[64,2,8,1024]{3,2,1,0:T(8,128)(2,1)S(1)} all-to-all(bf16[64,2,8,1024]{3,2,1,0:T(8,128)(2,1)S(1)} %dispatch.1), channel_id=1, replica_groups=mesh['rep'=8,'exp'=64] {'exp'}, dimensions={0} | all-to-all | bytes 4194304 | tf_op jit(solution)/shard_map/all_to_all | solution.py:198
  88.2 0.0 all-gather.3.cloned.1.call-done
  88.2 11.1 %experts_step.1 = (bf16[8,3,128,768]{3,2,1,0:T(8,128)(2,1)}, bf16[64,2,8,1024]{3,2,1,0:T(8,128)(2,1)}) custom-call(bf16[64,2,8,1024]{3,2,1,0:T(8,128)(2,1)S(1)} %all_to_all.10.xc_ref, bf16[8,3,128,768]{3,2,1,0:T(8,128)(2,1)} %bitcast.14), custom_call_target="tpu_custom_call" | custom-call | tf_op jit(solution)/shard_map/experts_step/pallas_call | solution.py:199
  99.4 0.0 reduce-scatter.2.cloned.1.call-update
  99.4 0.0 copy-start
  99.4 0.0 copy-start.1
  99.4 62.1 %all_to_all.11.back_ref = bf16[64,2,8,1024]{3,2,1,0:T(8,128)(2,1)S(1)} all-to-all(bf16[64,2,8,1024]{3,2,1,0:T(8,128)(2,1)} %get-tuple-element.12), channel_id=1, replica_groups=mesh['rep'=8,'exp'=64] {'exp'}, dimensions={0} | all-to-all | bytes 4194304 | tf_op jit(solution)/shard_map/all_to_all | solution.py:214
  161.5 0.0 reduce-scatter.2.cloned.1.call-done
  161.5 0.0 copy-done
  161.5 0.0 copy-done.1
  161.5 2.7 %finish.1 = (bf16[128,1024]{1,0:T(8,128)(2,1)}, bf16[128,1024]{1,0:T(8,128)(2,1)}, bf16[128,768]{1,0:T(8,128)(2,1)}, bf16[128,768]{1,0:T(8,128)(2,1)}, bf16[768,128]{1,0:T(8,128)(2,1)}) custom-call(s32[2,128]{1,0:T(2,128)S(1)} %bitcast.11, f32[2,128]{1,0:T(2,128)S(1)} %bitcast.13, bf16[64,2,8,1024]{3,2,1,0:T(8,128)(2,1)S(1)} %all_to_all.11.back_ref, ...), custom_call_target="tpu_custom_call" | custom-call | tf_op jit(solution)/shard_map/finish/pallas_call | solution.py:215
Async XLA Ops:
  7.2 81.1 %all-gather.3.cloned.1.call-start = ((), (), s32[]{:S(2)}) async-start(), calls=%async_computation.4 | async-start | bytes 5308416 | tf_op jit(solution)/shard_map/all_gather | solution.py:186
  20.3 141.2 %reduce-scatter.2.cloned.1.call-start = ((), (), s32[]{:S(2)}) async-start(), calls=%async_computation.3 | async-start | bytes 5308416 | tf_op jit(solution)/shard_map/reduce_scatter | solution.py:213
  99.4 62.1 %copy-start = (s32[128,2]{0,1:T(2,128)S(1)}, s32[128,2]{0,1:T(2,128)}, u32[]{:S(2)}) copy-start(s32[128,2]{0,1:T(2,128)} %param.9) | copy-start | bytes 3076
  99.4 62.1 %copy-start.1 = (f32[128,2]{0,1:T(2,128)S(1)}, f32[128,2]{0,1:T(2,128)}, u32[]{:S(2)}) copy-start(f32[128,2]{0,1:T(2,128)} %param.10) | copy-start | bytes 3076
Sparse Core Ops, SparseCore 0:
  20.4 67.5 all-gather.2
  99.5 61.4 reduce-scatter.1

commit v3 on v2

--- a/solution.py
+++ b/solution.py
@@ -52,14 +52,21 @@
         c.wait()
 
 
-def pack_weights(gate_hbm, up_hbm, down_hbm, out_hbm, down, turned, sems):
-    fetch = copy(down_hbm, down, sems.at[0])
-    fetch.start()
-    rest = run([copy(gate_hbm, out_hbm.at[0], sems.at[1]), copy(up_hbm, out_hbm.at[1], sems.at[2])])
-    fetch.wait()
-    turned[...] = down[...].T
-    rest += run([copy(turned, out_hbm.at[2], sems.at[3])])
-    drain(rest)
+def pack_weights(gate_hbm, up_hbm, down_hbm, out_hbm, flat, down, sems):
+    fetch = run(
+        [
+            copy(down_hbm, down, sems.at[2]),
+            copy(gate_hbm, flat.at[0], sems.at[0]),
+            copy(up_hbm, flat.at[1], sems.at[1]),
+        ]
+    )
+    fetch[0].wait()
+    flat[2] = down[...].T
+    store = run([copy(flat.at[2], out_hbm.at[2], sems.at[2])])
+    for i in range(2):
+        fetch[i + 1].wait()
+        store += run([copy(flat.at[i], out_hbm.at[i], sems.at[i])])
+    drain(store)
 
 
 def slot_onehots(ids_ref, experts, capacity):
@@ -142,23 +149,30 @@
 
 
 def finish(replicas):
-    def body(
-        ids_ref, cw_ref, back_ref, red_hbm, mixed_ref, grad_ref, gate_ref, up_ref, down_ref, red, sems
-    ):
-        fetch = run([copy(red_hbm, red, sems.at[0])])
+    def body(ids_ref, cw_ref, back_ref, red_hbm, *rest):
+        outs, (red, mixed, grad, scaled, turned, in_sems, out_sems) = rest[:5], rest[5:]
+        mixed_hbm, grad_hbm, gate_hbm, up_hbm, down_hbm = outs
+        fetch = run([copy(red_hbm.at[i], red.at[i], in_sems.at[i]) for i in range(3)])
         experts, _, capacity, features = back_ref.shape
         top, rows = ids_ref.shape
         picks = [p.astype(BF16) for p in slot_onehots(ids_ref, experts, capacity)]
+        pending = []
+
+        def store(value, index, source, target):
+            source[...] = value
+            pending.extend(run([copy(source, target, out_sems.at[index])]))
+
+        dx = back_ref[:, 1].reshape(experts * capacity, features)
+        store(tn(picks[0] + picks[1], dx).astype(BF16), 1, grad, grad_hbm)
+        drain(fetch)
+        store((red[2].astype(F32) / replicas).astype(BF16).T, 4, turned, down_hbm)
+        store((red[0].astype(F32) / replicas).astype(BF16), 2, scaled.at[0], gate_hbm)
+        store((red[1].astype(F32) / replicas).astype(BF16), 3, scaled.at[1], up_hbm)
         o = back_ref[:, 0].reshape(experts * capacity, features)
-        dx = back_ref[:, 1].reshape(experts * capacity, features)
         column = jnp.concatenate([cw_ref[...], jnp.zeros((8 - top, rows), F32)], axis=0).T
-        mixed = sum(column[:, k : k + 1] * tn(p, o) for k, p in enumerate(picks))
-        mixed_ref[...] = mixed.astype(BF16)
-        grad_ref[...] = tn(picks[0] + picks[1], dx).astype(BF16)
-        drain(fetch)
-        gate_ref[...] = (red[0].astype(F32) / replicas).astype(BF16)
-        up_ref[...] = (red[1].astype(F32) / replicas).astype(BF16)
-        down_ref[...] = (red[2].astype(F32) / replicas).astype(BF16).T
+        total = sum(column[:, k : k + 1] * tn(p, o) for k, p in enumerate(picks))
+        store(total.astype(BF16), 0, mixed, mixed_hbm)
+        drain(pending)
 
     return body
 
@@ -181,7 +195,7 @@
         "pack_weights",
         in_specs=[HBM] * 3,
         out_specs=HBM,
-        scratch_shapes=[scratch((ff, part), BF16), scratch((part, ff), BF16), sems((4,))],
+        scratch_shapes=[scratch((3, part, ff), BF16), scratch((ff, part), BF16), sems((3,))],
     )(*in_hbm(gate_weight[0], up_weight[0], down_weight[0]))
     weights = lax.all_gather(packed, "rep", axis=0)
     wire = (groups, 2, capacity, features)
@@ -214,12 +228,14 @@
     back = lax.all_to_all(results, "exp", split_axis=0, concat_axis=0, tiled=True)
     mixed, token_grad, gate_grad, up_grad, down_grad = call(
         finish(replicas),
-        (sds((tok_rows, features), BF16),) * 2
-        + (sds((part, ff), BF16), sds((part, ff), BF16), sds((ff, part), BF16)),
+        (pltpu.HBM((tok_rows, features), BF16),) * 2
+        + (pltpu.HBM((part, ff), BF16), pltpu.HBM((part, ff), BF16), pltpu.HBM((ff, part), BF16)),
         "finish",
         in_specs=[VMEM, VMEM, VMEM, HBM],
-        out_specs=(VMEM,) * 5,
-        scratch_shapes=[scratch((3, part, ff), BF16), sems((1,))],
+        out_specs=(HBM,) * 5,
+        scratch_shapes=[scratch((3, part, ff), BF16)]
+        + [scratch((tok_rows, features), BF16)] * 2
+        + [scratch((2, part, ff), BF16), scratch((ff, part), BF16), sems((3,)), sems((5,))],
     )(ids, cw, back, *in_hbm(reduced))
     return (mixed, token_grad, gate_grad[None], up_grad[None], down_grad[None])
 

time: 171 us -> 161 us (0.942)
  Pallas kernels: 28.9 us -> 17.5 us
    pallas_call x1, Pallas kernels: 13.1 us -> 1.91 us  [per_device(): call(pack_weights, pltpu.HBM((3, part, ff), BF16), 'pack_weights', in_spe...]
  transfers between devices with their start and end apart: 2 -> 2, of which waited for: 0 -> 1; matrix products, arithmetic and copies ran while one was open for 0% -> 0% of each run, Pallas kernels for 1% -> 1%
where the time goes in v3:
time: 161 us; the launch traced here: 160 us
  blocking collectives  128 us (80%)
  Pallas kernels  17.5 us (11%)
  between operations  14.1 us (9%)
    all_to_all x1, blocking collectives, per_device(): lax.all_to_all(sent, 'exp', split_axis=0, concat_axis=0, tiled=True)  65.9 us
    all_to_all x1, blocking collectives, per_device(): lax.all_to_all(results, 'exp', split_axis=0, concat_axis=0, tiled=True)  62.3 us
    pallas_call x1, Pallas kernels, per_device(): call(experts_step, (pltpu.HBM((replicas, 3, part, ff), BF16), pltpu.HBM(w...  11.1 us
  transfers between devices with their start and end apart: 2, of which 1 were waited for; matrix products, arithmetic and copies ran while one was open for 0% of the time, Pallas kernels for 1%

profile of v3, /device:TPU:1, one launch (start us, length us, event | category | flops | bytes accessed | tf_op | source)
XLA Modules:
  0.0 160.5 jit_solution(772555748689204295)
XLA Ops:
  7.2 0.0 all-gather.3.cloned.1.call-start
  7.2 1.9 %pack_weights.1 = bf16[3,128,768]{2,1,0:T(8,128)(2,1)} custom-call(bf16[128,768]{1,0:T(8,128)(2,1)} %bitcast.16, bf16[128,768]{1,0:T(8,128)(2,1)} %bitcast.17, bf16[768,128]{1,0:T(8,128)(2,1)} %bitcast.18), custom_call_target="tpu_custom_call" | custom-call | tf_op jit(solution)/shard_map/pack_weights/pallas_call | solution.py:192
  9.1 0.0 all-gather.3.cloned.1.call-update
  9.2 0.0 reduce-scatter.2.cloned.1.call-start
  9.2 2.0 %dispatch.1 = bf16[64,2,8,1024]{3,2,1,0:T(8,128)(2,1)S(1)} custom-call(s32[2,128]{1,0:T(2,128)} %bitcast.10, f32[2,128]{1,0:T(2,128)} %bitcast.12, bf16[128,1024]{1,0:T(8,128)(2,1)} %tok_hbm.1, bf16[128,1024]{1,0:T(8,128)(2,1)} %cot_hbm.1), custom_call_target="tpu_custom_call" | custom-call | tf_op jit(solution)/shard_map/dispatch/pallas_call | solution.py:202
  11.2 65.9 %all_to_all.10.xc_ref = bf16[64,2,8,1024]{3,2,1,0:T(8,128)(2,1)S(1)} all-to-all(bf16[64,2,8,1024]{3,2,1,0:T(8,128)(2,1)S(1)} %dispatch.1), channel_id=1, replica_groups=mesh['rep'=8,'exp'=64] {'exp'}, dimensions={0} | all-to-all | bytes 4194304 | tf_op jit(solution)/shard_map/all_to_all | solution.py:212
  77.1 0.5 all-gather.3.cloned.1.call-done
  77.7 11.1 %experts_step.1 = (bf16[8,3,128,768]{3,2,1,0:T(8,128)(2,1)}, bf16[64,2,8,1024]{3,2,1,0:T(8,128)(2,1)}) custom-call(bf16[64,2,8,1024]{3,2,1,0:T(8,128)(2,1)S(1)} %all_to_all.10.xc_ref, bf16[8,3,128,768]{3,2,1,0:T(8,128)(2,1)} %bitcast.14), custom_call_target="tpu_custom_call" | custom-call | tf_op jit(solution)/shard_map/experts_step/pallas_call | solution.py:213
  88.8 0.0 reduce-scatter.2.cloned.1.call-update
  88.8 0.0 copy-start
  88.8 0.0 copy-start.1
  88.8 62.3 %all_to_all.11.back_ref = bf16[64,2,8,1024]{3,2,1,0:T(8,128)(2,1)S(1)} all-to-all(bf16[64,2,8,1024]{3,2,1,0:T(8,128)(2,1)} %get-tuple-element.12), channel_id=1, replica_groups=mesh['rep'=8,'exp'=64] {'exp'}, dimensions={0} | all-to-all | bytes 4194304 | tf_op jit(solution)/shard_map/all_to_all | solution.py:228
  151.1 0.0 reduce-scatter.2.cloned.1.call-done
  151.1 0.0 copy-done
  151.1 0.0 copy-done.1
  151.1 2.5 %finish.1 = (bf16[128,1024]{1,0:T(8,128)(2,1)}, bf16[128,1024]{1,0:T(8,128)(2,1)}, bf16[128,768]{1,0:T(8,128)(2,1)}, bf16[128,768]{1,0:T(8,128)(2,1)}, bf16[768,128]{1,0:T(8,128)(2,1)}) custom-call(s32[2,128]{1,0:T(2,128)S(1)} %bitcast.11, f32[2,128]{1,0:T(2,128)S(1)} %bitcast.13, bf16[64,2,8,1024]{3,2,1,0:T(8,128)(2,1)S(1)} %all_to_all.11.back_ref, ...), custom_call_target="tpu_custom_call" | custom-call | tf_op jit(solution)/shard_map/finish/pallas_call | solution.py:229
Async XLA Ops:
  7.2 70.5 %all-gather.3.cloned.1.call-start = ((), (), s32[]{:S(2)}) async-start(), calls=%async_computation.4 | async-start | bytes 5308416 | tf_op jit(solution)/shard_map/all_gather | solution.py:200
  9.2 141.9 %reduce-scatter.2.cloned.1.call-start = ((), (), s32[]{:S(2)}) async-start(), calls=%async_computation.3 | async-start | bytes 5308416 | tf_op jit(solution)/shard_map/reduce_scatter | solution.py:227
  88.8 62.3 %copy-start = (s32[128,2]{0,1:T(2,128)S(1)}, s32[128,2]{0,1:T(2,128)}, u32[]{:S(2)}) copy-start(s32[128,2]{0,1:T(2,128)} %param.9) | copy-start | bytes 3076
  88.8 62.3 %copy-start.1 = (f32[128,2]{0,1:T(2,128)S(1)}, f32[128,2]{0,1:T(2,128)}, u32[]{:S(2)}) copy-start(f32[128,2]{0,1:T(2,128)} %param.10) | copy-start | bytes 3076
Sparse Core Ops, SparseCore 0:
  10.1 67.5 all-gather.2
  88.9 61.6 reduce-scatter.1

commit v4 on v3

--- a/solution.py
+++ b/solution.py
@@ -7,7 +7,7 @@
 
 F32 = jnp.float32
 BF16 = jnp.bfloat16
-VMEM_BYTES = 50 * 1024 * 1024
+VMEM_BYTES = 40 * 1024 * 1024
 
 
 def nn(a, b):
@@ -106,9 +106,8 @@
     return body
 
 
-def experts_step(
-    xc_ref, w_hbm, grads_hbm, out_hbm, w, g, out, hidden, dg, du, in_sems, grad_sems, out_sems
-):
+def expert_grads(xc_ref, w_hbm, grads_hbm, mid_hbm, w, g, mid, in_sems, out_sems, mid_sems):
+    hidden, dg, du = (mid.at[i] for i in range(3))
     groups, _, capacity, features = xc_ref.shape
     reps, _, part, ff = w_hbm.shape
     rows = groups * capacity
@@ -116,35 +115,60 @@
     weight = lambda i: w[i].reshape(features, ff)
     x = lambda: xc_ref[:, 0].reshape(rows, features)
     c = lambda: xc_ref[:, 1].reshape(rows, features)
+    pending = []
+    half = reps // 2
+
+    def keep(i, value):
+        mid[i] = value.astype(BF16)
+        pending.extend(run([copy(mid.at[i], mid_hbm.at[i], mid_sems.at[i])]))
+
+    def store(i, left, right):
+        for h in range(2):
+            block = slice(h * half, (h + 1) * half)
+            cols = slice(h * half * part, (h + 1) * half * part)
+            g[i, block] = tn(left()[:, cols], right[...]).astype(BF16).reshape(half, part, ff)
+            pending.extend(run([copy(g.at[i, block], grads_hbm.at[block, i], out_sems.at[i, h])]))
+
     fetch[0].wait()
     gate = nn(x(), weight(0))
     fetch[1].wait()
     up = nn(x(), weight(1))
+    sigma = jax.nn.sigmoid(gate)
+    swish = gate * sigma
+    keep(0, swish * up)
+    store(2, c, hidden)
     fetch[2].wait()
     dh = nn(c(), weight(2))
-    sigma = jax.nn.sigmoid(gate)
-    swish = gate * sigma
-    hidden[...] = (swish * up).astype(BF16)
-    dg[...] = (dh * up * sigma * (1.0 + gate * (1.0 - sigma))).astype(BF16)
-    du[...] = (dh * swish).astype(BF16)
+    keep(1, dh * up * sigma * (1.0 + gate * (1.0 - sigma)))
+    keep(2, dh * swish)
+    store(0, x, dg)
+    store(1, x, du)
+    drain(pending)
+
+
+def expert_rows(w_hbm, mid_hbm, out_hbm, w, mid, out, in_sems, out_sems, mid_sems):
+    hidden, dg, du = (mid.at[i] for i in range(3))
+    groups, _, capacity, features = out_hbm.shape
+    ff = w_hbm.shape[3]
+    fetch = [copy(w_hbm.at[:, i], w.at[i], in_sems.at[i]) for i in range(3)]
+    some = [copy(mid_hbm.at[i], mid.at[i], mid_sems.at[i]) for i in range(3)]
+    run([some[0], fetch[2], some[1], some[2], fetch[0], fetch[1]])
+    weight = lambda i: w[i].reshape(features, ff)
     pending = []
-    half = reps // 2
-    for i, (left, right) in enumerate(((x, dg), (x, du), (c, hidden))):
-        for h in range(2):
-            block = slice(h * half, (h + 1) * half)
-            cols = slice(h * half * part, (h + 1) * half * part)
-            g[i, block] = tn(left()[:, cols], right[...]).astype(BF16).reshape(half, part, ff)
-            pending += run([copy(g.at[i, block], grads_hbm.at[block, i], grad_sems.at[i, h])])
     half = groups // 2
+
+    def store(k, h, value):
+        block = slice(h * half, (h + 1) * half)
+        out[block, k] = value.astype(BF16).reshape(half, capacity, features)
+        pending.extend(run([copy(out.at[block, k], out_hbm.at[block, k], out_sems.at[k, h])]))
+
+    span = [slice(h * half * capacity, (h + 1) * half * capacity) for h in range(2)]
+    drain([some[0], fetch[2]])
     for h in range(2):
-        block = slice(h * half, (h + 1) * half)
-        some = slice(h * half * capacity, (h + 1) * half * capacity)
-        dx = nt(dg[some], weight(0)) + nt(du[some], weight(1))
-        out[block, 1] = dx.astype(BF16).reshape(half, capacity, features)
-        pending += run([copy(out.at[block, 1], out_hbm.at[block, 1], out_sems.at[1, h])])
-        o = nt(hidden[some], weight(2))
-        out[block, 0] = o.astype(BF16).reshape(half, capacity, features)
-        pending += run([copy(out.at[block, 0], out_hbm.at[block, 0], out_sems.at[0, h])])
+        store(0, h, nt(hidden[span[h]], weight(2)))
+    drain(some[1:] + fetch[:2])
+    for h in range(2):
+        store(1, h, nt(dg[span[h]], weight(0)) + nt(du[span[h]], weight(1)))
     drain(pending)
 
 
@@ -210,21 +234,31 @@
         + [sems((4,))],
     )(*in_hbm(ids, cw, tokens, cotangent))
     received = lax.all_to_all(sent, "exp", split_axis=0, concat_axis=0, tiled=True)
-    grads, results = call(
-        experts_step,
-        (pltpu.HBM((replicas, 3, part, ff), BF16), pltpu.HBM(wire, BF16)),
-        "experts_step",
+    grads, mid = call(
+        expert_grads,
+        (pltpu.HBM((replicas, 3, part, ff), BF16), pltpu.HBM((3, rows, ff), BF16)),
+        "expert_grads",
         in_specs=[VMEM, HBM],
         out_specs=(HBM, HBM),
+        scratch_shapes=[scratch((3, replicas, part, ff), BF16)] * 2
+        + [scratch((3, rows, ff), BF16), sems((3,)), sems((3, 2)), sems((3,))],
+    )(received, *in_hbm(weights))
+    reduced = lax.psum_scatter(grads, "rep", scatter_dimension=0)
+    results = call(
+        expert_rows,
+        pltpu.HBM(wire, BF16),
+        "expert_rows",
+        in_specs=[HBM, HBM],
+        out_specs=HBM,
         scratch_shapes=[
             scratch((3, replicas, part, ff), BF16),
-            scratch((3, replicas, part, ff), BF16),
+            scratch((3, rows, ff), BF16),
             scratch(wire, BF16),
-        ]
-        + [scratch((rows, ff), BF16)] * 3
-        + [sems((3,)), sems((3, 2)), sems((2, 2))],
-    )(received, *in_hbm(weights))
-    reduced = lax.psum_scatter(grads, "rep", scatter_dimension=0)
+            sems((3,)),
+            sems((2, 2)),
+            sems((3,)),
+        ],
+    )(*in_hbm(weights, mid))
     back = lax.all_to_all(results, "exp", split_axis=0, concat_axis=0, tiled=True)
     mixed, token_grad, gate_grad, up_grad, down_grad = call(
         finish(replicas),

time: 161 us -> 164 us (1.019)
  Pallas kernels: 17.5 us -> 21.1 us
    pallas_call x1 -> x2, Pallas kernels: 11.1 us -> 14.6 us  [the longest x1 8.85 us: per_device(): call(expert_grads, (pltpu.HBM((replicas, 3, part, ff), BF16), pltpu.HBM((...]
  transfers between devices with their start and end apart: 2 -> 2, of which waited for: 1 -> 1; matrix products, arithmetic and copies ran while one was open for 0% -> 0% of each run, Pallas kernels for 1% -> 5%
where the time goes in v4:
time: 164 us
  blocking collectives  128 us (78%)
  Pallas kernels  21.1 us (13%)
  between operations  14.1 us (9%)
    all_to_all x1, blocking collectives, per_device(): lax.all_to_all(sent, 'exp', split_axis=0, concat_axis=0, tiled=True)  65.9 us
    all_to_all x1, blocking collectives, per_device(): lax.all_to_all(results, 'exp', split_axis=0, concat_axis=0, tiled=True)  62.3 us
    pallas_call x1, Pallas kernels, per_device(): call(expert_grads, (pltpu.HBM((replicas, 3, part, ff), BF16), pltpu.HBM((...  8.85 us
    pallas_call x1, Pallas kernels, per_device(): call(expert_rows, pltpu.HBM(wire, BF16), 'expert_rows', in_specs=[HBM, HB...  5.8 us
  transfers between devices with their start and end apart: 2, of which 1 were waited for; matrix products, arithmetic and copies ran while one was open for 0% of the time, Pallas kernels for 5%

profile of v4, /device:TPU:1, one launch (start us, length us, event | category | flops | bytes accessed | tf_op | source)
XLA Modules:
  0.0 164.0 jit_solution(9924008111388153458)
XLA Ops:
  7.2 0.0 all-gather.3.cloned.1.call-start
  7.2 1.9 %pack_weights.1 = bf16[3,128,768]{2,1,0:T(8,128)(2,1)} custom-call(bf16[128,768]{1,0:T(8,128)(2,1)} %bitcast.17, bf16[128,768]{1,0:T(8,128)(2,1)} %bitcast.18, bf16[768,128]{1,0:T(8,128)(2,1)} %bitcast.19), custom_call_target="tpu_custom_call" | custom-call | tf_op jit(solution)/shard_map/pack_weights/pallas_call | solution.py:216
  9.1 0.0 all-gather.3.cloned.1.call-update
  9.2 0.0 reduce-scatter.2.cloned.1.call-start
  9.2 2.0 %dispatch.1 = bf16[64,2,8,1024]{3,2,1,0:T(8,128)(2,1)S(1)} custom-call(s32[2,128]{1,0:T(2,128)} %bitcast.10, f32[2,128]{1,0:T(2,128)} %bitcast.12, bf16[128,1024]{1,0:T(8,128)(2,1)} %tok_hbm.1, bf16[128,1024]{1,0:T(8,128)(2,1)} %cot_hbm.1), custom_call_target="tpu_custom_call" | custom-call | tf_op jit(solution)/shard_map/dispatch/pallas_call | solution.py:226
  11.2 65.9 %all_to_all.10.xc_ref = bf16[64,2,8,1024]{3,2,1,0:T(8,128)(2,1)S(1)} all-to-all(bf16[64,2,8,1024]{3,2,1,0:T(8,128)(2,1)S(1)} %dispatch.1), channel_id=1, replica_groups=mesh['rep'=8,'exp'=64] {'exp'}, dimensions={0} | all-to-all | bytes 4194304 | tf_op jit(solution)/shard_map/all_to_all | solution.py:236
  77.1 0.5 all-gather.3.cloned.1.call-done
  77.7 8.8 %expert_grads.1 = (bf16[8,3,128,768]{3,2,1,0:T(8,128)(2,1)}, bf16[3,512,768]{2,1,0:T(8,128)(2,1)}) custom-call(bf16[64,2,8,1024]{3,2,1,0:T(8,128)(2,1)S(1)} %all_to_all.10.xc_ref, bf16[8,3,128,768]{3,2,1,0:T(8,128)(2,1)} %bitcast.14), custom_call_target="tpu_custom_call" | custom-call | tf_op jit(solution)/shard_map/expert_grads/pallas_call | solution.py:237
  86.5 0.0 reduce-scatter.2.cloned.1.call-update
  86.5 5.8 %expert_rows.1 = bf16[64,2,8,1024]{3,2,1,0:T(8,128)(2,1)} custom-call(bf16[8,3,128,768]{3,2,1,0:T(8,128)(2,1)} %bitcast.15, bf16[3,512,768]{2,1,0:T(8,128)(2,1)} %get-tuple-element.12.mid_hbm), custom_call_target="tpu_custom_call" | custom-call | tf_op jit(solution)/shard_map/expert_rows/pallas_call | solution.py:247
  92.3 0.0 copy-start
  92.3 0.0 copy-start.1
  92.4 62.3 %all_to_all.11.back_ref = bf16[64,2,8,1024]{3,2,1,0:T(8,128)(2,1)S(1)} all-to-all(bf16[64,2,8,1024]{3,2,1,0:T(8,128)(2,1)} %expert_rows.1), channel_id=1, replica_groups=mesh['rep'=8,'exp'=64] {'exp'}, dimensions={0} | all-to-all | bytes 4194304 | tf_op jit(solution)/shard_map/all_to_all | solution.py:262
  154.6 0.0 reduce-scatter.2.cloned.1.call-done
  154.6 0.0 copy-done
  154.6 0.0 copy-done.1
  154.6 2.5 %finish.1 = (bf16[128,1024]{1,0:T(8,128)(2,1)}, bf16[128,1024]{1,0:T(8,128)(2,1)}, bf16[128,768]{1,0:T(8,128)(2,1)}, bf16[128,768]{1,0:T(8,128)(2,1)}, bf16[768,128]{1,0:T(8,128)(2,1)}) custom-call(s32[2,128]{1,0:T(2,128)S(1)} %bitcast.11, f32[2,128]{1,0:T(2,128)S(1)} %bitcast.13, bf16[64,2,8,1024]{3,2,1,0:T(8,128)(2,1)S(1)} %all_to_all.11.back_ref, ...), custom_call_target="tpu_custom_call" | custom-call | tf_op jit(solution)/shard_map/finish/pallas_call | solution.py:263
Async XLA Ops:
  7.2 70.5 %all-gather.3.cloned.1.call-start = ((), (), s32[]{:S(2)}) async-start(), calls=%async_computation.4 | async-start | bytes 5308416 | tf_op jit(solution)/shard_map/all_gather | solution.py:224
  9.2 145.5 %reduce-scatter.2.cloned.1.call-start = ((), (), s32[]{:S(2)}) async-start(), calls=%async_computation.3 | async-start | bytes 5308416 | tf_op jit(solution)/shard_map/reduce_scatter | solution.py:246
  92.3 62.3 %copy-start = (s32[128,2]{0,1:T(2,128)S(1)}, s32[128,2]{0,1:T(2,128)}, u32[]{:S(2)}) copy-start(s32[128,2]{0,1:T(2,128)} %param.9) | copy-start | bytes 3076
  92.3 62.3 %copy-start.1 = (f32[128,2]{0,1:T(2,128)S(1)}, f32[128,2]{0,1:T(2,128)}, u32[]{:S(2)}) copy-start(f32[128,2]{0,1:T(2,128)} %param.10) | copy-start | bytes 3076
Sparse Core Ops, SparseCore 0:
  10.1 67.5 all-gather.2
  86.7 61.6 reduce-scatter.1

commit v5 on v3

--- a/solution.py
+++ b/solution.py
@@ -78,19 +78,22 @@
     )
     before = nn(sum(hot).astype(BF16), earlier.astype(BF16))
     place = lax.broadcasted_iota(jnp.int32, (experts * capacity, rows), 0)
-    picks = []
+    spots = []
     for k in range(top):
         slot = jnp.sum(before * hot[k], axis=0, keepdims=True).astype(jnp.int32)
-        picks.append(place == ids_ref[k : k + 1, :] * capacity + slot)
-    return picks
+        spots.append(ids_ref[k : k + 1, :] * capacity + slot)
+    return spots, [place == spot for spot in spots]
 
 
 def dispatch(experts, capacity):
-    def body(ids_hbm, cw_hbm, tok_hbm, cot_hbm, out_ref, ids_ref, cw_ref, tok, cot, sems):
+    def body(ids_hbm, cw_hbm, tok_hbm, cot_hbm, out_ref, table_ref, ids_ref, cw_ref, tok, cot, sems):
         small = run([copy(ids_hbm, ids_ref, sems.at[2]), copy(cw_hbm, cw_ref, sems.at[3])])
         fetch = run([copy(tok_hbm, tok, sems.at[0]), copy(cot_hbm, cot, sems.at[1])])
         drain(small)
-        picks = slot_onehots(ids_ref, experts, capacity)
+        spots, picks = slot_onehots(ids_ref, experts, capacity)
+        top, rows = ids_ref.shape
+        lines = [spot.astype(F32) for spot in spots] + [cw_ref[...]]
+        table_ref[...] = jnp.concatenate(lines + [jnp.zeros((8 - 2 * top, rows), F32)], axis=0).T
         row_weight = sum(
             jnp.sum(jnp.where(p, cw_ref[k : k + 1, :], 0.0), axis=1, keepdims=True)
             for k, p in enumerate(picks)
@@ -149,13 +152,14 @@
 
 
 def finish(replicas):
-    def body(ids_ref, cw_ref, back_ref, red_hbm, *rest):
+    def body(table_ref, back_ref, red_hbm, *rest):
         outs, (red, mixed, grad, scaled, turned, in_sems, out_sems) = rest[:5], rest[5:]
         mixed_hbm, grad_hbm, gate_hbm, up_hbm, down_hbm = outs
         fetch = run([copy(red_hbm.at[i], red.at[i], in_sems.at[i]) for i in range(3)])
         experts, _, capacity, features = back_ref.shape
-        top, rows = ids_ref.shape
-        picks = [p.astype(BF16) for p in slot_onehots(ids_ref, experts, capacity)]
+        table = table_ref[...]
+        place = lax.broadcasted_iota(jnp.int32, (table.shape[0], experts * capacity), 1)
+        picks = [(place == table[:, k : k + 1].astype(jnp.int32)).astype(BF16) for k in range(2)]
         pending = []
 
         def store(value, index, source, target):
@@ -163,14 +167,13 @@
             pending.extend(run([copy(source, target, out_sems.at[index])]))
 
         dx = back_ref[:, 1].reshape(experts * capacity, features)
-        store(tn(picks[0] + picks[1], dx).astype(BF16), 1, grad, grad_hbm)
+        store(nn(picks[0] + picks[1], dx).astype(BF16), 1, grad, grad_hbm)
         drain(fetch)
         store((red[2].astype(F32) / replicas).astype(BF16).T, 4, turned, down_hbm)
         store((red[0].astype(F32) / replicas).astype(BF16), 2, scaled.at[0], gate_hbm)
         store((red[1].astype(F32) / replicas).astype(BF16), 3, scaled.at[1], up_hbm)
         o = back_ref[:, 0].reshape(experts * capacity, features)
-        column = jnp.concatenate([cw_ref[...], jnp.zeros((8 - top, rows), F32)], axis=0).T
-        total = sum(column[:, k : k + 1] * tn(p, o) for k, p in enumerate(picks))
+        total = sum(table[:, k + 2 : k + 3] * nn(p, o) for k, p in enumerate(picks))
         store(total.astype(BF16), 0, mixed, mixed_hbm)
         drain(pending)
 
@@ -199,12 +202,12 @@
     )(*in_hbm(gate_weight[0], up_weight[0], down_weight[0]))
     weights = lax.all_gather(packed, "rep", axis=0)
     wire = (groups, 2, capacity, features)
-    sent = call(
+    sent, table = call(
         dispatch(groups, capacity),
-        sds(wire, BF16),
+        (sds(wire, BF16), sds((tok_rows, 8), F32)),
         "dispatch",
         in_specs=[HBM] * 4,
-        out_specs=VMEM,
+        out_specs=(VMEM, VMEM),
         scratch_shapes=[scratch(ids.shape, jnp.int32), scratch(cw.shape, F32)]
         + [scratch(tokens.shape, BF16)] * 2
         + [sems((4,))],
@@ -231,12 +234,12 @@
         (pltpu.HBM((tok_rows, features), BF16),) * 2
         + (pltpu.HBM((part, ff), BF16), pltpu.HBM((part, ff), BF16), pltpu.HBM((ff, part), BF16)),
         "finish",
-        in_specs=[VMEM, VMEM, VMEM, HBM],
+        in_specs=[VMEM, VMEM, HBM],
         out_specs=(HBM,) * 5,
         scratch_shapes=[scratch((3, part, ff), BF16)]
         + [scratch((tok_rows, features), BF16)] * 2
         + [scratch((2, part, ff), BF16), scratch((ff, part), BF16), sems((3,)), sems((5,))],
-    )(ids, cw, back, *in_hbm(reduced))
+    )(table, back, *in_hbm(reduced))
     return (mixed, token_grad, gate_grad[None], up_grad[None], down_grad[None])
 
 

time: 161 us -> 161 us (level)
  no operation moved by 1% of the time
where the time goes in v5:
time: 161 us; the launch traced here: 160 us
  blocking collectives  128 us (80%)
  Pallas kernels  17.5 us (11%)
  between operations  14.1 us (9%)
    all_to_all x1, blocking collectives, per_device(): lax.all_to_all(sent, 'exp', split_axis=0, concat_axis=0, tiled=True)  65.9 us
    all_to_all x1, blocking collectives, per_device(): lax.all_to_all(results, 'exp', split_axis=0, concat_axis=0, tiled=True)  62.3 us
    pallas_call x1, Pallas kernels, per_device(): call(experts_step, (pltpu.HBM((replicas, 3, part, ff), BF16), pltpu.HBM(w...  11.1 us
  transfers between devices with their start and end apart: 2, of which 1 were waited for; matrix products, arithmetic and copies ran while one was open for 0% of the time, Pallas kernels for 1%

profile of v5, /device:TPU:1, one launch (start us, length us, event | category | flops | bytes accessed | tf_op | source)
XLA Modules:
  0.0 160.4 jit_solution(7863525349952717995)
XLA Ops:
  7.2 0.0 all-gather.3.cloned.1.call-start
  7.2 1.9 %pack_weights.1 = bf16[3,128,768]{2,1,0:T(8,128)(2,1)} custom-call(bf16[128,768]{1,0:T(8,128)(2,1)} %bitcast.12, bf16[128,768]{1,0:T(8,128)(2,1)} %bitcast.13, bf16[768,128]{1,0:T(8,128)(2,1)} %bitcast.14), custom_call_target="tpu_custom_call" | custom-call | tf_op jit(solution)/shard_map/pack_weights/pallas_call | solution.py:195
  9.1 0.0 all-gather.3.cloned.1.call-update
  9.1 0.0 reduce-scatter.2.cloned.1.call-start
  9.2 2.0 %dispatch.1 = (bf16[64,2,8,1024]{3,2,1,0:T(8,128)(2,1)S(1)}, f32[128,8]{1,0:T(8,128)S(1)}) custom-call(s32[2,128]{1,0:T(2,128)} %bitcast.15, f32[2,128]{1,0:T(2,128)} %bitcast.16, bf16[128,1024]{1,0:T(8,128)(2,1)} %tok_hbm.1, bf16[128,1024]{1,0:T(8,128)(2,1)} %cot_hbm.1), custom_call_target="tpu_custom_call" | custom-call | tf_op jit(solution)/shard_map/dispatch/pallas_call | solution.py:205
  11.2 65.9 %all_to_all.10.xc_ref = bf16[64,2,8,1024]{3,2,1,0:T(8,128)(2,1)S(1)} all-to-all(bf16[64,2,8,1024]{3,2,1,0:T(8,128)(2,1)S(1)} %get-tuple-element.15), channel_id=1, replica_groups=mesh['rep'=8,'exp'=64] {'exp'}, dimensions={0} | all-to-all | bytes 4194304 | tf_op jit(solution)/shard_map/all_to_all | solution.py:215
  77.1 0.5 all-gather.3.cloned.1.call-done
  77.7 11.1 %experts_step.1 = (bf16[8,3,128,768]{3,2,1,0:T(8,128)(2,1)}, bf16[64,2,8,1024]{3,2,1,0:T(8,128)(2,1)}) custom-call(bf16[64,2,8,1024]{3,2,1,0:T(8,128)(2,1)S(1)} %all_to_all.10.xc_ref, bf16[8,3,128,768]{3,2,1,0:T(8,128)(2,1)} %bitcast.10), custom_call_target="tpu_custom_call" | custom-call | tf_op jit(solution)/shard_map/experts_step/pallas_call | solution.py:216
  88.8 0.0 reduce-scatter.2.cloned.1.call-update
  88.8 62.3 %all_to_all.11.back_ref = bf16[64,2,8,1024]{3,2,1,0:T(8,128)(2,1)S(1)} all-to-all(bf16[64,2,8,1024]{3,2,1,0:T(8,128)(2,1)} %get-tuple-element.16), channel_id=1, replica_groups=mesh['rep'=8,'exp'=64] {'exp'}, dimensions={0} | all-to-all | bytes 4194304 | tf_op jit(solution)/shard_map/all_to_all | solution.py:231
  151.1 0.0 reduce-scatter.2.cloned.1.call-done
  151.1 2.4 %finish.1 = (bf16[128,1024]{1,0:T(8,128)(2,1)}, bf16[128,1024]{1,0:T(8,128)(2,1)}, bf16[128,768]{1,0:T(8,128)(2,1)}, bf16[128,768]{1,0:T(8,128)(2,1)}, bf16[768,128]{1,0:T(8,128)(2,1)}) custom-call(f32[128,8]{1,0:T(8,128)S(1)} %get-tuple-element.14.table_ref, bf16[64,2,8,1024]{3,2,1,0:T(8,128)(2,1)S(1)} %all_to_all.11.back_ref, bf16[3,128,768]{2,1,0:T(8,128)(2,1)} %bitcast.11), custom_call_target="tpu_custom_call" | custom-call | tf_op jit(solution)/shard_map/finish/pallas_call | solution.py:232
Async XLA Ops:
  7.2 70.5 %all-gather.3.cloned.1.call-start = ((), (), s32[]{:S(2)}) async-start(), calls=%async_computation.4 | async-start | bytes 5308416 | tf_op jit(solution)/shard_map/all_gather | solution.py:203
  9.1 141.9 %reduce-scatter.2.cloned.1.call-start = ((), (), s32[]{:S(2)}) async-start(), calls=%async_computation.3 | async-start | bytes 5308416 | tf_op jit(solution)/shard_map/reduce_scatter | solution.py:230
Sparse Core Ops, SparseCore 0:
  10.1 67.5 all-gather.2
  88.9 61.6 reduce-scatter.1

commit v6 on v5

--- a/solution.py
+++ b/solution.py
@@ -200,7 +200,8 @@
         out_specs=HBM,
         scratch_shapes=[scratch((3, part, ff), BF16), scratch((ff, part), BF16), sems((3,))],
     )(*in_hbm(gate_weight[0], up_weight[0], down_weight[0]))
-    weights = lax.all_gather(packed, "rep", axis=0)
+    weights = lax.all_gather(packed.reshape(3 * part, ff), "rep", axis=0, tiled=True)
+    weights = weights.reshape(replicas, 3, part, ff)
     wire = (groups, 2, capacity, features)
     sent, table = call(
         dispatch(groups, capacity),
@@ -227,7 +228,9 @@
         + [scratch((rows, ff), BF16)] * 3
         + [sems((3,)), sems((3, 2)), sems((2, 2))],
     )(received, *in_hbm(weights))
-    reduced = lax.psum_scatter(grads, "rep", scatter_dimension=0)
+    grads = grads.reshape(replicas * 3 * part, ff)
+    reduced = lax.psum_scatter(grads, "rep", scatter_dimension=0, tiled=True)
+    reduced = reduced.reshape(3, part, ff)
     back = lax.all_to_all(results, "exp", split_axis=0, concat_axis=0, tiled=True)
     mixed, token_grad, gate_grad, up_grad, down_grad = call(
         finish(replicas),

time: 161 us -> 161 us (level)
  no operation moved by 1% of the time
where the time goes in v6:
time: 161 us; the launch traced here: 160 us
  blocking collectives  128 us (80%)
  Pallas kernels  17.5 us (11%)
  between operations  14.1 us (9%)
    all_to_all x1, blocking collectives, per_device(): lax.all_to_all(sent, 'exp', split_axis=0, concat_axis=0, tiled=True)  65.9 us
    all_to_all x1, blocking collectives, per_device(): lax.all_to_all(results, 'exp', split_axis=0, concat_axis=0, tiled=True)  62.3 us
    pallas_call x1, Pallas kernels, per_device(): call(experts_step, (pltpu.HBM((replicas, 3, part, ff), BF16), pltpu.HBM(w...  11.1 us
  transfers between devices with their start and end apart: 2, of which 1 were waited for; matrix products, arithmetic and copies ran while one was open for 0% of the time, Pallas kernels for 1%

profile of v6, /device:TPU:1, one launch (start us, length us, event | category | flops | bytes accessed | tf_op | source)
XLA Modules:
  0.0 160.4 jit_solution(7556202198881189744)
XLA Ops:
  7.2 0.0 all-gather.2.cloned.1.call-start
  7.2 1.9 %pack_weights.1 = bf16[3,128,768]{2,1,0:T(8,128)(2,1)} custom-call(bf16[128,768]{1,0:T(8,128)(2,1)} %bitcast.16, bf16[128,768]{1,0:T(8,128)(2,1)} %bitcast.17, bf16[768,128]{1,0:T(8,128)(2,1)} %bitcast.18), custom_call_target="tpu_custom_call" | custom-call | tf_op jit(solution)/shard_map/pack_weights/pallas_call | solution.py:195
  9.1 0.0 all-gather.2.cloned.1.call-update
  9.1 0.0 reduce-scatter.2.cloned.1.call-start
  9.2 2.0 %dispatch.1 = (bf16[64,2,8,1024]{3,2,1,0:T(8,128)(2,1)S(1)}, f32[128,8]{1,0:T(8,128)S(1)}) custom-call(s32[2,128]{1,0:T(2,128)} %bitcast.19, f32[2,128]{1,0:T(2,128)} %bitcast.20, bf16[128,1024]{1,0:T(8,128)(2,1)} %tok_hbm.1, bf16[128,1024]{1,0:T(8,128)(2,1)} %cot_hbm.1), custom_call_target="tpu_custom_call" | custom-call | tf_op jit(solution)/shard_map/dispatch/pallas_call | solution.py:206
  11.2 65.9 %all_to_all.10.xc_ref = bf16[64,2,8,1024]{3,2,1,0:T(8,128)(2,1)S(1)} all-to-all(bf16[64,2,8,1024]{3,2,1,0:T(8,128)(2,1)S(1)} %get-tuple-element.15), channel_id=1, replica_groups=mesh['rep'=8,'exp'=64] {'exp'}, dimensions={0} | all-to-all | bytes 4194304 | tf_op jit(solution)/shard_map/all_to_all | solution.py:216
  77.1 0.5 all-gather.2.cloned.1.call-done
  77.7 11.1 %experts_step.1 = (bf16[8,3,128,768]{3,2,1,0:T(8,128)(2,1)}, bf16[64,2,8,1024]{3,2,1,0:T(8,128)(2,1)}) custom-call(bf16[64,2,8,1024]{3,2,1,0:T(8,128)(2,1)S(1)} %all_to_all.10.xc_ref, bf16[8,3,128,768]{3,2,1,0:T(8,128)(2,1)} %bitcast.13), custom_call_target="tpu_custom_call" | custom-call | tf_op jit(solution)/shard_map/experts_step/pallas_call | solution.py:217
  88.8 0.0 reduce-scatter.2.cloned.1.call-update
  88.8 62.3 %all_to_all.11.back_ref = bf16[64,2,8,1024]{3,2,1,0:T(8,128)(2,1)S(1)} all-to-all(bf16[64,2,8,1024]{3,2,1,0:T(8,128)(2,1)} %get-tuple-element.16), channel_id=1, replica_groups=mesh['rep'=8,'exp'=64] {'exp'}, dimensions={0} | all-to-all | bytes 4194304 | tf_op jit(solution)/shard_map/all_to_all | solution.py:234
  151.1 0.0 reduce-scatter.2.cloned.1.call-done
  151.1 2.4 %finish.1 = (bf16[128,1024]{1,0:T(8,128)(2,1)}, bf16[128,1024]{1,0:T(8,128)(2,1)}, bf16[128,768]{1,0:T(8,128)(2,1)}, bf16[128,768]{1,0:T(8,128)(2,1)}, bf16[768,128]{1,0:T(8,128)(2,1)}) custom-call(f32[128,8]{1,0:T(8,128)S(1)} %get-tuple-element.14.table_ref, bf16[64,2,8,1024]{3,2,1,0:T(8,128)(2,1)S(1)} %all_to_all.11.back_ref, bf16[3,128,768]{2,1,0:T(8,128)(2,1)} %bitcast.15), custom_call_target="tpu_custom_call" | custom-call | tf_op jit(solution)/shard_map/finish/pallas_call | solution.py:235
Async XLA Ops:
  7.2 70.5 %all-gather.2.cloned.1.call-start = ((), (), s32[]{:S(2)}) async-start(), calls=%async_computation.3 | async-start | bytes 5308416 | tf_op jit(solution)/shard_map/all_gather | solution.py:203
  9.1 141.9 %reduce-scatter.2.cloned.1.call-start = ((), (), s32[]{:S(2)}) async-start(), calls=%async_computation.4 | async-start | bytes 5308416 | tf_op jit(solution)/shard_map/reduce_scatter | solution.py:232
Sparse Core Ops, SparseCore 0:
  10.1 67.5 all-gather.1
  88.9 61.6 reduce-scatter.1

commit v7 on v6

--- a/solution.py
+++ b/solution.py
@@ -151,30 +151,32 @@
     drain(pending)
 
 
-def finish(replicas):
-    def body(table_ref, back_ref, red_hbm, *rest):
-        outs, (red, mixed, grad, scaled, turned, in_sems, out_sems) = rest[:5], rest[5:]
-        mixed_hbm, grad_hbm, gate_hbm, up_hbm, down_hbm = outs
-        fetch = run([copy(red_hbm.at[i], red.at[i], in_sems.at[i]) for i in range(3)])
-        experts, _, capacity, features = back_ref.shape
-        table = table_ref[...]
-        place = lax.broadcasted_iota(jnp.int32, (table.shape[0], experts * capacity), 1)
-        picks = [(place == table[:, k : k + 1].astype(jnp.int32)).astype(BF16) for k in range(2)]
-        pending = []
-
-        def store(value, index, source, target):
-            source[...] = value
-            pending.extend(run([copy(source, target, out_sems.at[index])]))
-
-        dx = back_ref[:, 1].reshape(experts * capacity, features)
-        store(nn(picks[0] + picks[1], dx).astype(BF16), 1, grad, grad_hbm)
-        drain(fetch)
-        store((red[2].astype(F32) / replicas).astype(BF16).T, 4, turned, down_hbm)
-        store((red[0].astype(F32) / replicas).astype(BF16), 2, scaled.at[0], gate_hbm)
-        store((red[1].astype(F32) / replicas).astype(BF16), 3, scaled.at[1], up_hbm)
-        o = back_ref[:, 0].reshape(experts * capacity, features)
-        total = sum(table[:, k + 2 : k + 3] * nn(p, o) for k, p in enumerate(picks))
-        store(total.astype(BF16), 0, mixed, mixed_hbm)
+def combine(table_ref, back_ref, mixed_hbm, grad_hbm, mixed, grad, sems):
+    experts, _, capacity, features = back_ref.shape
+    table = table_ref[...]
+    place = lax.broadcasted_iota(jnp.int32, (table.shape[0], experts * capacity), 1)
+    picks = [(place == table[:, k : k + 1].astype(jnp.int32)).astype(BF16) for k in range(2)]
+    dx = back_ref[:, 1].reshape(experts * capacity, features)
+    grad[...] = nn(picks[0] + picks[1], dx).astype(BF16)
+    pending = run([copy(grad, grad_hbm, sems.at[1])])
+    o = back_ref[:, 0].reshape(experts * capacity, features)
+    total = sum(table[:, k + 2 : k + 3] * nn(p, o) for k, p in enumerate(picks))
+    mixed[...] = total.astype(BF16)
+    drain(pending + run([copy(mixed, mixed_hbm, sems.at[0])]))
+
+
+def average_grads(replicas):
+    def body(red_hbm, gate_hbm, up_hbm, down_hbm, red, scaled, turned, in_sems, out_sems):
+        fetch = [copy(red_hbm.at[i], red.at[i], in_sems.at[i]) for i in range(3)]
+        run([fetch[2], fetch[0], fetch[1]])
+        mean = lambda i: (red[i].astype(F32) / replicas).astype(BF16)
+        fetch[2].wait()
+        turned[...] = mean(2).T
+        pending = run([copy(turned, down_hbm, out_sems.at[2])])
+        for i, target in enumerate((gate_hbm, up_hbm)):
+            fetch[i].wait()
+            scaled[i] = mean(i)
+            pending += run([copy(scaled.at[i], target, out_sems.at[i])])
         drain(pending)
 
     return body
@@ -232,17 +234,28 @@
     reduced = lax.psum_scatter(grads, "rep", scatter_dimension=0, tiled=True)
     reduced = reduced.reshape(3, part, ff)
     back = lax.all_to_all(results, "exp", split_axis=0, concat_axis=0, tiled=True)
-    mixed, token_grad, gate_grad, up_grad, down_grad = call(
-        finish(replicas),
-        (pltpu.HBM((tok_rows, features), BF16),) * 2
-        + (pltpu.HBM((part, ff), BF16), pltpu.HBM((part, ff), BF16), pltpu.HBM((ff, part), BF16)),
-        "finish",
-        in_specs=[VMEM, VMEM, HBM],
-        out_specs=(HBM,) * 5,
-        scratch_shapes=[scratch((3, part, ff), BF16)]
-        + [scratch((tok_rows, features), BF16)] * 2
-        + [scratch((2, part, ff), BF16), scratch((ff, part), BF16), sems((3,)), sems((5,))],
-    )(table, back, *in_hbm(reduced))
+    mixed, token_grad = call(
+        combine,
+        (pltpu.HBM((tok_rows, features), BF16),) * 2,
+        "combine",
+        in_specs=[VMEM, VMEM],
+        out_specs=(HBM, HBM),
+        scratch_shapes=[scratch((tok_rows, features), BF16)] * 2 + [sems((2,))],
+    )(table, back)
+    gate_grad, up_grad, down_grad = call(
+        average_grads(replicas),
+        (pltpu.HBM((part, ff), BF16), pltpu.HBM((part, ff), BF16), pltpu.HBM((ff, part), BF16)),
+        "average_grads",
+        in_specs=[HBM],
+        out_specs=(HBM,) * 3,
+        scratch_shapes=[
+            scratch((3, part, ff), BF16),
+            scratch((2, part, ff), BF16),
+            scratch((ff, part), BF16),
+            sems((3,)),
+            sems((3,)),
+        ],
+    )(*in_hbm(reduced))
     return (mixed, token_grad, gate_grad[None], up_grad[None], down_grad[None])
 
 

time: 161 us -> 163 us (1.012)
    pallas_call x1 -> x2, Pallas kernels: 2.45 us -> 3.3 us  [the longest x1 1.89 us: per_device(): call(average_grads(replicas), (pltpu.HBM((part, ff), BF16), pltpu.HBM((pa...]
  transfers between devices with their start and end apart: 2 -> 2, of which waited for: 1 -> 1; matrix products, arithmetic and copies ran while one was open for 0% -> 0% of each run, Pallas kernels for 1% -> 2%
where the time goes in v7:
time: 163 us
  blocking collectives  128 us (79%)
  Pallas kernels  18.4 us (11%)
  between operations  14.1 us (9%)
    all_to_all x1, blocking collectives, per_device(): lax.all_to_all(sent, 'exp', split_axis=0, concat_axis=0, tiled=True)  65.9 us
    all_to_all x1, blocking collectives, per_device(): lax.all_to_all(results, 'exp', split_axis=0, concat_axis=0, tiled=True)  62.1 us
    pallas_call x1, Pallas kernels, per_device(): call(experts_step, (pltpu.HBM((replicas, 3, part, ff), BF16), pltpu.HBM(w...  11.1 us
  transfers between devices with their start and end apart: 2, of which 1 were waited for; matrix products, arithmetic and copies ran while one was open for 0% of the time, Pallas kernels for 2%

profile of v7, /device:TPU:1, one launch (start us, length us, event | category | flops | bytes accessed | tf_op | source)
XLA Modules:
  0.0 162.6 jit_solution(4527810955852057630)
XLA Ops:
  7.2 0.0 all-gather.2.cloned.1.call-start
  7.2 1.9 %pack_weights.1 = bf16[3,128,768]{2,1,0:T(8,128)(2,1)} custom-call(bf16[128,768]{1,0:T(8,128)(2,1)} %bitcast.16, bf16[128,768]{1,0:T(8,128)(2,1)} %bitcast.17, bf16[768,128]{1,0:T(8,128)(2,1)} %bitcast.18), custom_call_target="tpu_custom_call" | custom-call | tf_op jit(solution)/shard_map/pack_weights/pallas_call | solution.py:197
  9.1 0.0 all-gather.2.cloned.1.call-update
  9.2 0.0 reduce-scatter.2.cloned.1.call-start
  9.2 2.0 %dispatch.1 = (bf16[64,2,8,1024]{3,2,1,0:T(8,128)(2,1)S(1)}, f32[128,8]{1,0:T(8,128)S(1)}) custom-call(s32[2,128]{1,0:T(2,128)} %bitcast.19, f32[2,128]{1,0:T(2,128)} %bitcast.20, bf16[128,1024]{1,0:T(8,128)(2,1)} %tok_hbm.1, bf16[128,1024]{1,0:T(8,128)(2,1)} %cot_hbm.1), custom_call_target="tpu_custom_call" | custom-call | tf_op jit(solution)/shard_map/dispatch/pallas_call | solution.py:208
  11.3 65.9 %all_to_all.10.xc_ref = bf16[64,2,8,1024]{3,2,1,0:T(8,128)(2,1)S(1)} all-to-all(bf16[64,2,8,1024]{3,2,1,0:T(8,128)(2,1)S(1)} %get-tuple-element.15), channel_id=1, replica_groups=mesh['rep'=8,'exp'=64] {'exp'}, dimensions={0} | all-to-all | bytes 4194304 | tf_op jit(solution)/shard_map/all_to_all | solution.py:218
  77.1 0.5 all-gather.2.cloned.1.call-done
  77.7 11.1 %experts_step.1 = (bf16[8,3,128,768]{3,2,1,0:T(8,128)(2,1)}, bf16[64,2,8,1024]{3,2,1,0:T(8,128)(2,1)}) custom-call(bf16[64,2,8,1024]{3,2,1,0:T(8,128)(2,1)S(1)} %all_to_all.10.xc_ref, bf16[8,3,128,768]{3,2,1,0:T(8,128)(2,1)} %bitcast.13), custom_call_target="tpu_custom_call" | custom-call | tf_op jit(solution)/shard_map/experts_step/pallas_call | solution.py:219
  88.8 0.0 copy-start
  88.8 0.0 reduce-scatter.2.cloned.1.call-update
  88.8 1.6 copy-done
  90.4 62.1 %all_to_all.11.back_ref = bf16[64,2,8,1024]{3,2,1,0:T(8,128)(2,1)S(1)} all-to-all(bf16[64,2,8,1024]{3,2,1,0:T(8,128)(2,1)S(1)} %copy-done), channel_id=1, replica_groups=mesh['rep'=8,'exp'=64] {'exp'}, dimensions={0} | all-to-all | bytes 4194304 | tf_op jit(solution)/shard_map/all_to_all | solution.py:236
  152.4 1.4 combine.1
  153.9 0.0 reduce-scatter.2.cloned.1.call-done
  153.9 1.9 %average_grads.1 = (bf16[128,768]{1,0:T(8,128)(2,1)}, bf16[128,768]{1,0:T(8,128)(2,1)}, bf16[768,128]{1,0:T(8,128)(2,1)}) custom-call(bf16[3,128,768]{2,1,0:T(8,128)(2,1)} %bitcast.15), custom_call_target="tpu_custom_call" | custom-call | tf_op jit(solution)/shard_map/average_grads/pallas_call | solution.py:245
Async XLA Ops:
  7.2 70.5 %all-gather.2.cloned.1.call-start = ((), (), s32[]{:S(2)}) async-start(), calls=%async_computation.3 | async-start | bytes 5308416 | tf_op jit(solution)/shard_map/all_gather | solution.py:205
  9.2 144.7 %reduce-scatter.2.cloned.1.call-start = ((), (), s32[]{:S(2)}) async-start(), calls=%async_computation.4 | async-start | bytes 5308416 | tf_op jit(solution)/shard_map/reduce_scatter | solution.py:234
  88.8 1.6 copy-start
Sparse Core Ops, SparseCore 0:
  10.1 67.5 all-gather.1
  88.9 61.6 reduce-scatter.1
